TPU v7x, 32 devices: a whole 2x2x4 slice. The times are simulated.
32 devices in a mesh: lon: 4 (over z), head: 4 (over y, core), dp: 2 (over x).
Axes of the slice: x: 2, y: 2, z: 4, core: 2. Of those that a mesh axis runs over, the one named last changes fastest.
Arguments:
- queries: bfloat16 [2, 2048, 3072], P('dp', 'lon', 'head'), may hold values from -6 to 6
- key_heads: bfloat16 [2, 2048, 3072], P('dp', 'lon', 'head'), may hold values from -6 to 6
- value_heads: bfloat16 [2, 2048, 3072], P('dp', 'lon', 'head'), may hold values from -6 to 6
- out_grad: bfloat16 [2, 2048, 3072], P('dp', ('lon', 'head')), may hold values from -6 to 6
- out_weight: bfloat16 [3072, 3072], P('head'), may hold values from -0.109375 to 0.109375
- neighbours: int32 [8, 4], replicated, may hold values from 0 to 7, as said below
- slot_valid: int32 [8, 4], replicated, may hold values 0 or 1
Outputs:
- grad_queries: bfloat16 [2, 2048, 3072], P('dp', 'lon', 'head')
- grad_keys: bfloat16 [2, 2048, 3072], P('dp', 'lon', 'head')
- grad_values: bfloat16 [2, 2048, 3072], P('dp', 'lon', 'head')
- grad_weight: float32 [3072, 3072], P(('lon', 'dp'), 'head')
Inputs may be any that keep to these rules, and one draw needn't show every extreme that they name: neighbours[t, j] lies within 2 tiles of t around the closed loop of 8 tiles.
All inputs are finite; a program needn't handle non-finite values.
Results may differ from a plain program's by a relative error of at most 0.012.
The roundings to bfloat16 on the way count: a program that leaves them out, or rounds other values in their place, can miss the bound.
Values may be sent and summed in bfloat16 or wider, within the bound.
A program may use at most 128 MiB of HBM per device.

v0:
```python
import math

import jax
import jax.numpy as jnp
from jax import lax
from jax.sharding import PartitionSpec as P

HEAD_DIM = 128
TILE = 256


def passed_along(value, axis, steps):
    count = lax.axis_size(axis)
    pairs = [(source, (source + steps) % count) for source in range(count)]
    return lax.ppermute(value, axis, pairs)


def attend_head(query_tiles, key_tiles, value_tiles, grad_tiles, slot_tiles, slot_live):
    factor = 1.0 / math.sqrt(query_tiles.shape[-1])
    picked_keys = jnp.take(key_tiles, slot_tiles, axis=0)
    picked_values = jnp.take(value_tiles, slot_tiles, axis=0)
    scores = (
        jnp.einsum("qid,qsjd->qisj", query_tiles, picked_keys, preferred_element_type=jnp.float32)
        * factor
    )
    is_live = (slot_live > 0)[:, None, :, None]
    scores = jnp.where(is_live, scores, -jnp.inf)
    row_max = jnp.max(scores, axis=(2, 3), keepdims=True)
    raised = jnp.exp(scores - row_max)
    weights = raised / jnp.sum(raised, axis=(2, 3), keepdims=True)
    weights_low = weights.astype(jnp.bfloat16)
    attended = jnp.einsum(
        "qisj,qsjd->qid", weights_low, picked_values, preferred_element_type=jnp.float32
    ).astype(jnp.bfloat16)
    row_delta = jnp.sum(grad_tiles.astype(jnp.float32) * attended.astype(jnp.float32), axis=-1)
    grad_weights = jnp.einsum(
        "qid,qsjd->qisj", grad_tiles, picked_values, preferred_element_type=jnp.float32
    )
    grad_scores = (weights * (grad_weights - row_delta[:, :, None, None]) * factor).astype(
        jnp.bfloat16
    )
    grad_query = jnp.einsum(
        "qisj,qsjd->qid", grad_scores, picked_keys, preferred_element_type=jnp.float32
    ).astype(jnp.bfloat16)
    key_blocks = jnp.einsum(
        "qisj,qid->qsjd", grad_scores, query_tiles, preferred_element_type=jnp.float32
    )
    value_blocks = jnp.einsum(
        "qisj,qid->qsjd", weights_low, grad_tiles, preferred_element_type=jnp.float32
    )
    key_sums = jnp.zeros(key_tiles.shape, jnp.float32).at[slot_tiles].add(key_blocks)
    value_sums = jnp.zeros(value_tiles.shape, jnp.float32).at[slot_tiles].add(value_blocks)
    return (attended, grad_query, key_sums, value_sums)


def local(queries, key_heads, value_heads, out_grad, out_weight, neighbours, slot_valid):
    token_count = queries.shape[1]
    feature_count = queries.shape[2]
    head_count = feature_count // HEAD_DIM
    tiles_here = token_count // TILE
    lon_count = lax.axis_size("lon")
    tile_total = tiles_here * lon_count
    first_tile = lax.axis_index("lon") * tiles_here
    own_rows = lax.dynamic_slice_in_dim(neighbours, first_tile, tiles_here, 0)
    own_live = lax.dynamic_slice_in_dim(slot_valid, first_tile, tiles_here, 0)
    local_index = jnp.arange(tiles_here, dtype=jnp.int32)
    far_index = (own_rows - first_tile + tiles_here) % tile_total
    slot_tiles = jnp.concatenate([(local_index + tiles_here)[:, None], far_index], axis=1)
    slot_live = jnp.concatenate([jnp.ones((tiles_here, 1), jnp.int32), own_live], axis=1)
    gathered = lax.all_gather(out_grad, "head", axis=1, tiled=True)
    grad_rows = gathered[0]
    grad_attn = lax.dot_general(
        grad_rows, out_weight, (((1,), (1,)), ((), ())), preferred_element_type=jnp.float32
    ).astype(jnp.bfloat16)
    stacked = jnp.stack((key_heads[0], value_heads[0]))
    behind = passed_along(stacked, "lon", 1)
    beyond = passed_along(stacked, "lon", -1)
    extended = jnp.concatenate((behind, stacked, beyond), axis=1)

    def heads_first(matrix, row_count):
        return matrix.reshape(row_count // TILE, TILE, head_count, HEAD_DIM).transpose(2, 0, 1, 3)

    def tokens_first(blocks, row_count):
        return blocks.transpose(1, 2, 0, 3).reshape(row_count, feature_count)

    def per_head(head_parts):
        return attend_head(
            head_parts[0], head_parts[1], head_parts[2], head_parts[3], slot_tiles, slot_live
        )

    attended, grad_query, key_sums, value_sums = lax.map(
        per_head,
        (
            heads_first(queries[0], token_count),
            heads_first(extended[0], 3 * token_count),
            heads_first(extended[1], 3 * token_count),
            heads_first(grad_attn, token_count),
        ),
    )
    attn_out = tokens_first(attended, token_count)
    grad_pair = jnp.stack(
        (tokens_first(key_sums, 3 * token_count), tokens_first(value_sums, 3 * token_count))
    )
    from_beyond = passed_along(grad_pair[:, :token_count], "lon", -1)
    from_behind = passed_along(grad_pair[:, 2 * token_count :], "lon", 1)
    summed = (grad_pair[:, token_count : 2 * token_count] + from_beyond + from_behind).astype(
        jnp.bfloat16
    )
    grad_weight = lax.psum_scatter(
        lax.dot_general(
            grad_rows, attn_out, (((0,), (0,)), ((), ())), preferred_element_type=jnp.float32
        ),
        ("lon", "dp"),
        scatter_dimension=0,
        tiled=True,
    )
    grad_queries = tokens_first(grad_query, token_count)[None]
    return (grad_queries, summed[0][None], summed[1][None], grad_weight)


def solution(mesh):
    in_specs = (
        P("dp", "lon", "head"),
        P("dp", "lon", "head"),
        P("dp", "lon", "head"),
        P("dp", ("lon", "head"), None),
        P("head", None),
        P(),
        P(),
    )
    out_specs = (
        P("dp", "lon", "head"),
        P("dp", "lon", "head"),
        P("dp", "lon", "head"),
        P(("lon", "dp"), "head"),
    )
    return jax.shard_map(local, mesh=mesh, in_specs=in_specs, out_specs=out_specs, check_vma=False)
```

profile of v0, /device:TPU:0, one launch (start us, length us, event | category | flops | bytes accessed | tf_op | source)
XLA Modules:
  0.0 495.1 jit_solution(8115851102504979204)
XLA Ops:
  9.2 5.1 %collective-permute-start.1 = (bf16[2,512,768]{2,1,0:T(8,128)(2,1)S(1)}, bf16[2,512,768]{2,1,0:T(8,128)(2,1)}, u32[]{:S(2)}, u32[]{:S(2)}) collective-permute-start(bf16[2,512,768]{2,1,0:T(8,128)(2,1)S(1)} %constant_dynamic-update-slice_fusion), channel_id=1, source_target_pairs={{0,24},{8,0},{16,8},{24,16},{1,25},{9,1},{17,9},{25,17},{2,26},{10... | collective-permute-start | bytes 4718600 | tf_op jit(solution)/shard_map/ppermute | solution.py:15
  16.2 33.0 %collective-permute-done.1 = bf16[2,512,768]{2,1,0:T(8,128)(2,1)} collective-permute-done((bf16[2,512,768]{2,1,0:T(8,128)(2,1)S(1)}, bf16[2,512,768]{2,1,0:T(8,128)(2,1)}, u32[]{:S(2)}, u32[]{:S(2)}) %collective-permute-start.1) | collective-permute-done | bytes 1572896 | tf_op jit(solution)/shard_map/ppermute | solution.py:15
  49.1 33.6 %collective-permute-done = bf16[2,512,768]{2,1,0:T(8,128)(2,1)} collective-permute-done((bf16[2,512,768]{2,1,0:T(8,128)(2,1)S(1)}, bf16[2,512,768]{2,1,0:T(8,128)(2,1)}, u32[]{:S(2)}, u32[]{:S(2)}) %collective-permute-start) | collective-permute-done | bytes 1572896 | tf_op jit(solution)/shard_map/ppermute | solution.py:15
  84.7 2.4 fusion.38
  87.2 4.8 reshape_squeeze.11
  94.0 4.8 reshape_squeeze.10
  100.8 5.9 %fusion.33 = bf16[512,768]{1,0:T(8,128)(2,1)S(1)} fusion(bf16[768,3072]{1,0:T(8,128)(2,1)} %param.15, bf16[1,512,3072]{2,1,0:T(8,128)(2,1)} %all-gather.2.cloned.1.call-done), kind=kOutput, calls=%fused_computation.58 | convolution fusion | flops 2416312320 | bytes 8650752 | tf_op jit(solution)/shard_map/dot_general | solution.py:72
  108.1 108.8 %while.16 = (s32[]{:T(128)}, bf16[6,2,256,128]{2,3,1,0:T(8,128)(2,1)}, bf16[6,2,256,128]{3,2,1,0:T(8,128)(2,1)}, f32[6,6,256,128]{3,2,1,0:T(8,128)}, f32[6,6,256...) while((s32[]{:T(128)}, ...), condition=%wide.region_6.8_spmd, body=%wide.region_0.7_spmd.sunk | while | flops 1025375872 | bytes 44723276 | solution.py:91
  120.3 2.4 fusion.63
  156.6 2.4 fusion.63
  174.7 2.4 fusion.63
  192.9 2.4 fusion.63
  219.2 5.1 %convolution_bitcast_fusion.2 = f32[3072,768]{0,1:T(8,128)} fusion(bf16[512,768]{0,1:T(8,128)(2,1)S(1)} %bitcast.135, bf16[1,512,3072]{2,1,0:T(8,128)(2,1)S(1)} %copy-done.10), kind=kOutput, calls=%fused_computation.50 | convolution fusion | flops 2415919104 | bytes 13369344 | tf_op jit(solution)/shard_map/dot_general | solution.py:110
  224.3 8.0 %copy.42 = f32[6,256,6,128]{3,2,1,0:T(8,128)} copy(f32[6,256,6,128]{3,1,0,2:T(8,128)} %bitcast.131) | data formatting | bytes 9437184 | tf_op jit(solution)/shard_map/transpose | solution.py:84
  232.4 6.9 %stack_reshape.7 = f32[1,1536,768]{2,1,0:T(8,128)} reshape(f32[6,256,6,128]{3,2,1,0:T(8,128)} %copy.42) | data formatting | bytes 9437184 | tf_op jit(solution)/shard_map/stack;reshape | solution.py:101
  239.3 7.8 %copy.41 = f32[6,256,6,128]{3,2,1,0:T(8,128)} copy(f32[6,256,6,128]{3,1,0,2:T(8,128)} %bitcast.132) | data formatting | bytes 9437184 | tf_op jit(solution)/shard_map/transpose | solution.py:84
  247.1 6.9 %stack_reshape.6 = f32[1,1536,768]{2,1,0:T(8,128)} reshape(f32[6,256,6,128]{3,2,1,0:T(8,128)} %copy.41) | data formatting | bytes 9437184 | tf_op jit(solution)/shard_map/stack;reshape | solution.py:101
  254.0 2.9 constant_dynamic-update-slice_fusion.3
  258.2 3.2 fusion.37
  268.1 123.8 %collective-permute-done.2 = f32[2,512,768]{2,1,0:T(8,128)} collective-permute-done((f32[2,512,768]{2,1,0:T(8,128)}, f32[2,512,768]{2,1,0:T(8,128)}, u32[]{:S(2)}, u32[]{:S(2)}) %collective-permute-start.2) | collective-permute-done | bytes 3145760 | tf_op jit(solution)/shard_map/ppermute | solution.py:15
  391.9 63.2 %collective-permute-done.3 = f32[2,512,768]{2,1,0:T(8,128)} collective-permute-done((f32[2,512,768]{2,1,0:T(8,128)}, f32[2,512,768]{2,1,0:T(8,128)}, u32[]{:S(2)}, u32[]{:S(2)}) %collective-permute-start.3) | collective-permute-done | bytes 3145760 | tf_op jit(solution)/shard_map/ppermute | solution.py:15
  455.0 4.3 fusion.29
  460.6 25.1 %reduce-scatter.2.cloned.1.call-done = f32[384,768]{0,1:T(8,128)} async-done(((f32[3072,768]{0,1:T(8,128)}), f32[384,768]{0,1:T(8,128)}) %reduce-scatter.2.cloned.1.call-update) | async-done | bytes 1179664 | tf_op jit(solution)/shard_map/reduce_scatter | solution.py:109
  485.6 2.7 copy.45
  (268 shorter events, 120.8 us)
Async XLA Ops:
  7.2 7.2 %copy-start.9 = (s32[8,4]{0,1:T(4,128)S(1)}, s32[8,4]{0,1:T(4,128)}, u32[]{:S(2)}) copy-start(s32[8,4]{0,1:T(4,128)} %param.17) | copy-start | bytes 388
  7.2 7.2 %copy-start.8 = (s32[8,4]{0,1:T(4,128)S(1)}, s32[8,4]{0,1:T(4,128)}, u32[]{:S(2)}) copy-start(s32[8,4]{0,1:T(4,128)} %param.16) | copy-start | bytes 388
  7.2 7.4 %copy-start.7 = (bf16[1,512,768]{2,1,0:T(8,128)(2,1)S(1)}, bf16[1,512,768]{2,1,0:T(8,128)(2,1)}, u32[]{:S(2)}) copy-start(bf16[1,512,768]{2,1,0:T(8,128)(2,1)} %param.11) | copy-start | bytes 2359300
  7.2 93.6 %all-gather.2.cloned.1.call-start = ((), (), s32[]{:S(2)}) async-start(), calls=%async_computation.1 | async-start | bytes 3932160 | tf_op jit(solution)/shard_map/all_gather | solution.py:70
  7.9 477.7 %reduce-scatter.2.cloned.1.call-start = ((), (), s32[]{:S(2)}) async-start(), calls=%async_computation.2 | async-start | bytes 10616832 | tf_op jit(solution)/shard_map/reduce_scatter | solution.py:109
  9.2 39.9 %collective-permute-start.1 = (bf16[2,512,768]{2,1,0:T(8,128)(2,1)S(1)}, bf16[2,512,768]{2,1,0:T(8,128)(2,1)}, u32[]{:S(2)}, u32[]{:S(2)}) collective-permute-start(bf16[2,512,768]{2,1,0:T(8,128)(2,1)S(1)} %constant_dynamic-update-slice_fusion), channel_id=1, source_target_pairs={{0,24},{8,0},{16,8},{24,16},{1,25},{9,1},{17,9},{25,17},{2,26},{10... | collective-permute-start | bytes 4718600 | tf_op jit(solution)/shard_map/ppermute | solution.py:15
  14.3 68.4 %collective-permute-start = (bf16[2,512,768]{2,1,0:T(8,128)(2,1)S(1)}, bf16[2,512,768]{2,1,0:T(8,128)(2,1)}, u32[]{:S(2)}, u32[]{:S(2)}) collective-permute-start(bf16[2,512,768]{2,1,0:T(8,128)(2,1)S(1)} %constant_dynamic-update-slice_fusion), channel_id=1, source_target_pairs={{0,8},{8,16},{16,24},{24,0},{1,9},{9,17},{17,25},{25,1},{2,10},{10... | collective-permute-start | bytes 4718600 | tf_op jit(solution)/shard_map/ppermute | solution.py:15
  108.1 8.6 %copy-start.11 = (pred[2,5]{1,0:T(4,128)(4,1)}, pred[2,5]{1,0:T(4,128)(4,1)S(1)}, u32[]{:S(2)}) copy-start(pred[2,5]{1,0:T(4,128)(4,1)S(1)} %compare_and_fusion.2) | copy-start | bytes 34 | tf_op jit(solution)/shard_map/while
  110.4 4.1 copy-start.3
  118.6 4.1 copy-start.4
  126.3 8.6 %copy-start.11 = (pred[2,5]{1,0:T(4,128)(4,1)}, pred[2,5]{1,0:T(4,128)(4,1)S(1)}, u32[]{:S(2)}) copy-start(pred[2,5]{1,0:T(4,128)(4,1)S(1)} %compare_and_fusion.2) | copy-start | bytes 34 | tf_op jit(solution)/shard_map/while
  136.8 4.1 copy-start.4
  144.4 8.6 %copy-start.11 = (pred[2,5]{1,0:T(4,128)(4,1)}, pred[2,5]{1,0:T(4,128)(4,1)S(1)}, u32[]{:S(2)}) copy-start(pred[2,5]{1,0:T(4,128)(4,1)S(1)} %compare_and_fusion.2) | copy-start | bytes 34 | tf_op jit(solution)/shard_map/while
  154.9 4.1 copy-start.4
  162.5 8.6 %copy-start.11 = (pred[2,5]{1,0:T(4,128)(4,1)}, pred[2,5]{1,0:T(4,128)(4,1)S(1)}, u32[]{:S(2)}) copy-start(pred[2,5]{1,0:T(4,128)(4,1)S(1)} %compare_and_fusion.2) | copy-start | bytes 34 | tf_op jit(solution)/shard_map/while
  173.0 4.1 copy-start.4
  180.6 8.6 %copy-start.11 = (pred[2,5]{1,0:T(4,128)(4,1)}, pred[2,5]{1,0:T(4,128)(4,1)S(1)}, u32[]{:S(2)}) copy-start(pred[2,5]{1,0:T(4,128)(4,1)S(1)} %compare_and_fusion.2) | copy-start | bytes 34 | tf_op jit(solution)/shard_map/while
  191.2 4.1 copy-start.4
  198.8 8.6 %copy-start.11 = (pred[2,5]{1,0:T(4,128)(4,1)}, pred[2,5]{1,0:T(4,128)(4,1)S(1)}, u32[]{:S(2)}) copy-start(pred[2,5]{1,0:T(4,128)(4,1)S(1)} %compare_and_fusion.2) | copy-start | bytes 34 | tf_op jit(solution)/shard_map/while
  209.3 4.1 copy-start.4
  258.2 5.5 %copy-start = (f32[2,1536,768]{2,1,0:T(8,128)}, f32[2,1536,768]{2,1,0:T(8,128)S(1)}, u32[]{:S(2)}) copy-start(f32[2,1536,768]{2,1,0:T(8,128)S(1)} %constant_dynamic-update-slice_fusion.2) | copy-start | bytes 28311556
  258.2 7.6 %copy-start.5 = (bf16[6,2,256,128]{3,2,1,0:T(8,128)(2,1)S(1)}, bf16[6,2,256,128]{3,2,1,0:T(8,128)(2,1)}, u32[]{:S(2)}) copy-start(bf16[6,2,256,128]{3,2,1,0:T(8,128)(2,1)} %get-tuple-element.65) | copy-start | bytes 2359300
  263.7 128.2 %collective-permute-start.2 = (f32[2,512,768]{2,1,0:T(8,128)}, f32[2,512,768]{2,1,0:T(8,128)}, u32[]{:S(2)}, u32[]{:S(2)}) collective-permute-start(f32[2,512,768]{2,1,0:T(8,128)} %get-tuple-element.127), channel_id=1, source_target_pairs={{0,24},{8,0},{16,8},{24,16},{1,25},{9,1},{17,9},{25,17},{2,26},{10... | collective-permute-start | bytes 9437192 | tf_op jit(solution)/shard_map/ppermute | solution.py:15
  265.0 190.0 %collective-permute-start.3 = (f32[2,512,768]{2,1,0:T(8,128)}, f32[2,512,768]{2,1,0:T(8,128)}, u32[]{:S(2)}, u32[]{:S(2)}) collective-permute-start(f32[2,512,768]{2,1,0:T(8,128)} %get-tuple-element.128), channel_id=1, source_target_pairs={{0,8},{8,16},{16,24},{24,0},{1,9},{9,17},{17,25},{25,1},{2,10},{10... | collective-permute-start | bytes 9437192 | tf_op jit(solution)/shard_map/ppermute | solution.py:15
  (20 other events, 46.1 us)
Sparse Core Ops, SparseCore 0:
  9.6 31.2 all-gather.1
  224.5 261.1 reduce-scatter.1
where the time goes:
time: 497 us; the launch traced here: 495 us
  waiting for transfers between devices  279 us (56%)
  local copies, waits for them, and re-layouts  111 us (22%)
  matrix products  52.1 us (10%)
  other arithmetic  30.3 us (6%)
  between operations  14.2 us (3%)
  starting transfers between devices  7.21 us (1%)
    ppermute x4, waiting for transfers between devices, passed_along(): return lax.ppermute(value, axis, pairs)  254 us
    reduce_scatter x1, waiting for transfers between devices, local(): lax.psum_scatter(lax.dot_general(grad_rows, attn_out, (((0,), (0,)), ((),...  25.1 us
    transpose x3, local copies, waits for them, and re-layouts, tokens_first(): return blocks.transpose(1, 2, 0, 3).reshape(row_count, feature_count)  17.9 us
    dot_general x6, matrix products, attend_head(): jnp.einsum('qisj,qsjd->qid', grad_scores, picked_keys, preferred_element_...  14.4 us
    another operation x3, local copies, waits for them, and re-layouts, local(): jnp.stack((tokens_first(key_sums, 3 * token_count), tokens_first(value_su...  14.2 us
    unnamed x25, local copies, waits for them, and re-layouts  12.9 us
    dynamic_slice x18, local copies, waits for them, and re-layouts, local(): lax.map(per_head, (heads_first(queries[0], token_count), heads_first(exte...  12.8 us
    squeeze x12, local copies, waits for them, and re-layouts, local(): lax.map(per_head, (heads_first(queries[0], token_count), heads_first(exte...  12.6 us
  transfers between devices with their start and end apart: 6, of which 5 were waited for; matrix products, arithmetic and copies ran while one was open for 13% of the time, Pallas kernels for 0%

commit v1 on v0

v1 whole, which is shorter than its diff:
```python
import functools
import math

import jax
import jax.numpy as jnp
from jax import lax
from jax.experimental import pallas as pl
from jax.experimental.pallas import tpu as pltpu
from jax.sharding import PartitionSpec as P

HEAD_DIM = 128
TILE = 256
REACH = 2
CHUNK_HEADS = 2
NT = (((1,), (1,)), ((), ()))
NN = (((1,), (0,)), ((), ()))
TN = (((0,), (0,)), ((), ()))


def mul(a, b, dims):
    return lax.dot_general(a, b, dims, preferred_element_type=jnp.float32)


def shifted(value, axis, steps):
    count = lax.axis_size(axis)
    pairs = [(source, (source + steps) % count) for source in range(count)]
    return lax.ppermute(value, axis, pairs)


def flipped(value, axis, bit):
    count = lax.axis_size(axis)
    return lax.ppermute(value, axis, [(source, source ^ bit) for source in range(count)])


def attend_kernel(
    counts_ref,
    q_ref,
    k_ref,
    v_ref,
    g_ref,
    behind_ref,
    beyond_ref,
    dq_ref,
    att_ref,
    own_ref,
    to_behind_ref,
    to_beyond_ref,
    k_ext,
    v_ext,
    dk_ext,
    dv_ext,
):
    factor = 1.0 / math.sqrt(HEAD_DIM)
    rows = q_ref.shape[0]
    tiles = rows // TILE
    k_ext[0:rows] = behind_ref[0]
    k_ext[rows : 2 * rows] = k_ref[...]
    k_ext[2 * rows : 3 * rows] = beyond_ref[0]
    v_ext[0:rows] = behind_ref[1]
    v_ext[rows : 2 * rows] = v_ref[...]
    v_ext[2 * rows : 3 * rows] = beyond_ref[1]
    wide = 2 * REACH + 1
    seen = set()
    for i in range(tiles):
        here = slice(i * TILE, (i + 1) * TILE)
        q = q_ref[here]
        g = g_ref[here]
        spots = []
        for o in range(wide):
            at = (i + tiles - REACH + o) * TILE
            spots.append(slice(at, at + TILE))
        live = [counts_ref[i * wide + o] for o in range(wide)]
        scores = []
        top = None
        for o in range(wide):
            bias = jnp.where(live[o] > 0.0, 0.0, -jnp.inf)
            s = mul(k_ext[spots[o]], q, NT) * factor + bias
            scores.append(s)
            m = jnp.max(s, axis=0, keepdims=True)
            top = m if top is None else jnp.maximum(top, m)
        total = None
        raised = []
        for o in range(wide):
            e = jnp.exp(scores[o] - top)
            raised.append(e)
            part = jnp.sum(e, axis=0, keepdims=True) * live[o]
            total = part if total is None else total + part
        inverse = 1.0 / total
        weights = []
        att = None
        for o in range(wide):
            w = raised[o] * inverse
            weights.append(w)
            low = w.astype(jnp.bfloat16)
            part = mul(v_ext[spots[o]], low, TN) * live[o]
            att = part if att is None else att + part
            dv = mul(low, g, NN) * live[o]
            if spots[o].start in seen:
                dv_ext[spots[o]] += dv
            else:
                dv_ext[spots[o]] = dv
        att_rows = att.T.astype(jnp.bfloat16)
        att_ref[here] = att_rows
        g_turned = g.astype(jnp.float32).T
        delta = jnp.sum(
            g_turned * att.astype(jnp.bfloat16).astype(jnp.float32), axis=0, keepdims=True
        )
        dq = None
        for o in range(wide):
            dw = mul(v_ext[spots[o]], g, NT)
            ds = (weights[o] * (dw - delta) * factor).astype(jnp.bfloat16)
            part = mul(k_ext[spots[o]], ds, TN) * live[o]
            dq = part if dq is None else dq + part
            dk = mul(ds, q, NN) * live[o]
            if spots[o].start in seen:
                dk_ext[spots[o]] += dk
            else:
                dk_ext[spots[o]] = dk
            seen.add(spots[o].start)
        dq_ref[here] = dq.T.astype(jnp.bfloat16)
    for n, ext in ((0, dk_ext), (1, dv_ext)):
        to_behind_ref[n] = ext[0:rows].astype(jnp.bfloat16)
        own_ref[n] = ext[rows : 2 * rows]
        to_beyond_ref[n] = ext[2 * rows : 3 * rows].astype(jnp.bfloat16)


def attend(counts, q, k, v, g, behind, beyond, first_head, heads):
    rows = q.shape[0]
    cols = heads * HEAD_DIM
    whole = pl.BlockSpec((rows, HEAD_DIM), lambda h: (0, first_head + h))
    part = pl.BlockSpec((rows, HEAD_DIM), lambda h: (0, h))
    pair = pl.BlockSpec((2, rows, HEAD_DIM), lambda h: (0, 0, h))
    flops = 12 * rows * (2 * REACH + 1) * TILE * cols
    return pl.pallas_call(
        attend_kernel,
        grid=(heads,),
        in_specs=[
            pl.BlockSpec(memory_space=pltpu.SMEM),
            whole,
            whole,
            whole,
            whole,
            pair,
            pair,
        ],
        out_specs=[part, part, pair, pair, pair],
        out_shape=[
            jax.ShapeDtypeStruct((rows, cols), jnp.bfloat16),
            jax.ShapeDtypeStruct((rows, cols), jnp.bfloat16),
            jax.ShapeDtypeStruct((2, rows, cols), jnp.float32),
            jax.ShapeDtypeStruct((2, rows, cols), jnp.bfloat16),
            jax.ShapeDtypeStruct((2, rows, cols), jnp.bfloat16),
        ],
        scratch_shapes=[
            pltpu.VMEM((3 * rows, HEAD_DIM), jnp.bfloat16),
            pltpu.VMEM((3 * rows, HEAD_DIM), jnp.bfloat16),
            pltpu.VMEM((3 * rows, HEAD_DIM), jnp.float32),
            pltpu.VMEM((3 * rows, HEAD_DIM), jnp.float32),
        ],
        cost_estimate=pl.CostEstimate(
            flops=flops, bytes_accessed=20 * rows * cols * 2, transcendentals=rows * 1280 * heads
        ),
    )(counts, q, k, v, g, behind, beyond)


def halved(blocks, axis, dim):
    count = lax.axis_size(axis)
    me = lax.axis_index(axis)
    bit = 1
    while bit < count:
        mine = (me // bit) % 2
        shape = blocks.shape
        split = shape[:dim] + (shape[dim] // 2, 2) + shape[dim + 1 :]
        paired = blocks.reshape(split)
        kept = lax.dynamic_index_in_dim(paired, mine, dim + 1, keepdims=False)
        sent = lax.dynamic_index_in_dim(paired, 1 - mine, dim + 1, keepdims=False)
        arrived = flipped(sent.astype(jnp.bfloat16), axis, bit)
        blocks = kept + arrived.astype(jnp.float32)
        bit *= 2
    return blocks


def local(queries, key_heads, value_heads, out_grad, out_weight, neighbours, slot_valid):
    q, k, v = queries[0], key_heads[0], value_heads[0]
    rows, features = q.shape
    heads = features // HEAD_DIM
    tiles = rows // TILE
    lon_count = lax.axis_size("lon")
    dp_count = lax.axis_size("dp")
    head_count = lax.axis_size("head")
    tile_total = tiles * lon_count
    first_tile = lax.axis_index("lon") * tiles
    own_rows = lax.dynamic_slice_in_dim(neighbours, first_tile, tiles, 0)
    own_live = lax.dynamic_slice_in_dim(slot_valid, first_tile, tiles, 0)
    index = first_tile + jnp.arange(tiles, dtype=jnp.int32)
    offset = (own_rows - index[:, None] + REACH + tile_total) % tile_total
    span = jnp.arange(2 * REACH + 1, dtype=jnp.int32)
    named = (offset[:, :, None] == span) & (own_live > 0)[:, :, None]
    counts = jnp.sum(named.astype(jnp.float32), axis=1) + (span == REACH).astype(jnp.float32)
    counts = counts.reshape(-1)

    chunks = heads // CHUNK_HEADS
    cols = CHUNK_HEADS * HEAD_DIM
    behind, beyond = [], []
    for c in range(chunks):
        cut = slice(c * cols, (c + 1) * cols)
        stacked = jnp.stack((k[:, cut], v[:, cut]))
        behind.append(shifted(stacked, "lon", 1))
        beyond.append(shifted(stacked, "lon", -1))

    mine = out_grad[0]
    got = {0: mine}
    bit = head_count // 2
    while bit:
        for at in sorted(got):
            got[at ^ bit] = flipped(got[at], "head", bit)
        bit //= 2
    piece = mine.shape[0]
    me = lax.axis_index("head")
    grad_rows = jnp.zeros((rows, mine.shape[1]), mine.dtype)
    for at in sorted(got):
        grad_rows = lax.dynamic_update_slice_in_dim(grad_rows, got[at], (me ^ at) * piece, 0)
    grad_attn = mul(grad_rows, out_weight, NT).astype(jnp.bfloat16)

    dq, summed, grad_weight = [], [], []
    for c in range(chunks):
        part_q, att, own, to_behind, to_beyond = attend(
            counts, q, k, v, grad_attn, behind[c], beyond[c], c * CHUNK_HEADS, CHUNK_HEADS
        )
        dq.append(part_q)
        from_beyond = shifted(to_behind, "lon", -1)
        from_behind = shifted(to_beyond, "lon", 1)
        summed.append(
            (own + from_beyond.astype(jnp.float32) + from_behind.astype(jnp.float32)).astype(
                jnp.bfloat16
            )
        )
        term = mul(grad_rows, att, TN)
        blocks = term.reshape(lon_count, dp_count, -1, cols)
        blocks = halved(blocks, "dp", 1)
        blocks = halved(blocks, "lon", 0)
        grad_weight.append(blocks[0, 0])
    joined = jnp.concatenate(summed, axis=2)
    return (
        jnp.concatenate(dq, axis=1)[None],
        joined[0][None],
        joined[1][None],
        jnp.concatenate(grad_weight, axis=1),
    )


def solution(mesh):
    in_specs = (
        P("dp", "lon", "head"),
        P("dp", "lon", "head"),
        P("dp", "lon", "head"),
        P("dp", ("lon", "head"), None),
        P("head", None),
        P(),
        P(),
    )
    out_specs = (
        P("dp", "lon", "head"),
        P("dp", "lon", "head"),
        P("dp", "lon", "head"),
        P(("lon", "dp"), "head"),
    )
    return jax.shard_map(local, mesh=mesh, in_specs=in_specs, out_specs=out_specs, check_vma=False)
```

time: 497 us -> 196 us (0.39)
  waiting for transfers between devices: 279 us -> 102 us
  local copies, waits for them, and re-layouts: 111 us -> 9.57 us
  matrix products: 52.1 us -> 7.64 us
  Pallas kernels: 0 us -> 32 us
  starting transfers between devices: 7.21 us -> 33.3 us
  other arithmetic: 30.3 us -> 9.7 us
  between operations: 14.2 us -> 1.09 us
    ppermute x4 -> x24, waiting for transfers between devices: 254 us -> 102 us  [the longest x12 56.5 us: shifted(): return lax.ppermute(value, axis, pairs)]
    dot_general x38 -> x4, matrix products: 52.1 us -> 7.64 us  [mul(): return lax.dot_general(a, b, dims, preferred_element_type=jnp.float32)]
    pallas_call x0 -> x3, Pallas kernels: none -> 32 us  [attend(): pl.pallas_call(attend_kernel, grid=(heads,), in_specs=[pl.BlockSpec(memor...]
    ppermute x4 -> x24, starting transfers between devices: 7.13 us -> 33.3 us  [the longest x12 22.1 us: shifted(): return lax.ppermute(value, axis, pairs)]
    reduce_scatter x1 -> x0, waiting for transfers between devices: 25.1 us -> none  [local(): lax.psum_scatter(lax.dot_general(grad_rows, attn_out, (((0,), (0,)), ((),...]
    another operation x19 -> x1, local copies, waits for them, and re-layouts: 25.5 us -> 2.17 us  [local(): stacked = jnp.stack((k[:, cut], v[:, cut]))]
    scatter-add x12 -> x0, other arithmetic: 19.9 us -> none  [the longest x6 9.93 us: attend_head(): jnp.zeros(value_tiles.shape, jnp.float32).at[slot_tiles].add(value_blocks)]
    transpose x3 -> x0, local copies, waits for them, and re-layouts: 17.9 us -> none  [tokens_first(): return blocks.transpose(1, 2, 0, 3).reshape(row_count, feature_count)]
  transfers between devices with their start and end apart: 6 -> 24, of which waited for: 5 -> 13; matrix products, arithmetic and copies ran while one was open for 13% -> 13% of each run, Pallas kernels for 0% -> 16%
where the time goes in v1:
time: 196 us
  waiting for transfers between devices  102 us (52%)
  starting transfers between devices  33.3 us (17%)
  Pallas kernels  32 us (16%)
  other arithmetic  9.7 us (5%)
  local copies, waits for them, and re-layouts  9.57 us (5%)
  matrix products  7.64 us (4%)
    ppermute x12, waiting for transfers between devices, shifted(): return lax.ppermute(value, axis, pairs)  56.5 us
    ppermute x12, waiting for transfers between devices, flipped(): lax.ppermute(value, axis, [(source, source ^ bit) for source in range(cou...  46 us
    pallas_call x3, Pallas kernels, attend(): pl.pallas_call(attend_kernel, grid=(heads,), in_specs=[pl.BlockSpec(memor...  32 us
    ppermute x12, starting transfers between devices, shifted(): return lax.ppermute(value, axis, pairs)  22.1 us
    ppermute x12, starting transfers between devices, flipped(): lax.ppermute(value, axis, [(source, source ^ bit) for source in range(cou...  11.2 us
    dot_general x4, matrix products, mul(): return lax.dot_general(a, b, dims, preferred_element_type=jnp.float32)  7.64 us
  transfers between devices with their start and end apart: 24, of which 13 were waited for; matrix products, arithmetic and copies ran while one was open for 13% of the time, Pallas kernels for 16%

profile of v1, /device:TPU:0, one launch (start us, length us, event | category | flops | bytes accessed | tf_op | source)
XLA Modules:
  0.0 195.8 jit_solution(11262648276790466179)
XLA Ops:
  1.2 2.6 %collective-permute-start.1 = (bf16[128,3072]{1,0:T(8,128)(2,1)}, bf16[128,3072]{1,0:T(8,128)(2,1)}, u32[]{:S(2)}, u32[]{:S(2)}) collective-permute-start(bf16[128,3072]{1,0:T(8,128)(2,1)} %bitcast.96), channel_id=1, source_target_pairs={{0,4},{2,6},{4,0},{6,2},{1,5},{3,7},{5,1},{7,3},{8,12},{10,14},{12... | collective-permute-start | bytes 2359304 | tf_op jit(solution)/shard_map/ppermute | solution.py:32
  3.8 2.2 %slice_bitcast_fusion.4 = (bf16[1,512,256]{2,1,0:T(8,128)(2,1)S(1)}, bf16[1,512,256]{2,1,0:T(8,128)(2,1)S(1)}, bf16[1,512,256]{2,1,0:T(8,128)(2,1)S(1)}, bf16[1,...) fusion(bf16[512,768]{1,0:T(8,128)(2,1)} %bitcast.101, ...), kind=kLoop, calls=%fused_computation.38 | loop fusion | bytes 3145728 | tf_op jit(solution)/shard_map/stack | solution.py:207
  6.8 3.6 %collective-permute-start.6 = (bf16[2,512,256]{2,1,0:T(8,128)(2,1)}, bf16[2,512,256]{2,1,0:T(8,128)(2,1)}, u32[]{:S(2)}, u32[]{:S(2)}) collective-permute-start(bf16[2,512,256]{2,1,0:T(8,128)(2,1)} %pad_maximum_fusion.3), channel_id=1, source_target_pairs={{0,24},{8,0},{16,8},{24,16},{1,25},{9,1},{17,9},{25,17},{2,26},{10... | collective-permute-start | bytes 1572872 | tf_op jit(solution)/shard_map/ppermute | solution.py:27
  11.2 3.8 %collective-permute-start.8 = (bf16[2,512,256]{2,1,0:T(8,128)(2,1)}, bf16[2,512,256]{2,1,0:T(8,128)(2,1)}, u32[]{:S(2)}, u32[]{:S(2)}) collective-permute-start(bf16[2,512,256]{2,1,0:T(8,128)(2,1)} %pad_maximum_fusion.4), channel_id=1, source_target_pairs={{0,24},{8,0},{16,8},{24,16},{1,25},{9,1},{17,9},{25,17},{2,26},{10... | collective-permute-start | bytes 1572872 | tf_op jit(solution)/shard_map/ppermute | solution.py:27
  17.8 4.4 %collective-permute-done.1 = bf16[128,3072]{1,0:T(8,128)(2,1)} collective-permute-done((bf16[128,3072]{1,0:T(8,128)(2,1)}, bf16[128,3072]{1,0:T(8,128)(2,1)}, u32[]{:S(2)}, u32[]{:S(2)}) %collective-permute-start.1) | collective-permute-done | bytes 786464 | tf_op jit(solution)/shard_map/ppermute | solution.py:32
  30.4 15.1 %collective-permute-done.8.beyond_ref = bf16[2,512,256]{2,1,0:T(8,128)(2,1)} collective-permute-done((bf16[2,512,256]{2,1,0:T(8,128)(2,1)}, bf16[2,512,256]{2,1,0:T(8,128)(2,1)}, u32[]{:S(2)}, u32[]{:S(2)}) %collective-permute-start.8) | collective-permute-done | bytes 524320 | tf_op jit(solution)/shard_map/ppermute | solution.py:27
  46.4 3.6 %convolution_convert_fusion.g_ref = bf16[512,768]{1,0:T(8,128)(2,1)} fusion(bf16[512,3072]{1,0:T(8,128)(2,1)S(1)} %constant_dynamic-update-slice_fusion, bf16[768,3072]{1,0:T(8,128)(2,1)S(1)} %copy-done.10), kind=kOutput, calls=%fused_computation.7 | convolution fusion | flops 2416312320 | bytes 8650752 | tf_op jit(solution)/shard_map/dot_general | solution.py:21
  50.0 7.7 %collective-permute-done.7.behind_ref = bf16[2,512,256]{2,1,0:T(8,128)(2,1)} collective-permute-done((bf16[2,512,256]{2,1,0:T(8,128)(2,1)}, bf16[2,512,256]{2,1,0:T(8,128)(2,1)}, u32[]{:S(2)}, u32[]{:S(2)}) %collective-permute-start.7) | collective-permute-done | bytes 524320 | tf_op jit(solution)/shard_map/ppermute | solution.py:27
  57.7 10.7 %shard_map.104 = (bf16[512,256]{1,0:T(8,128)(2,1)}, bf16[512,256]{1,0:T(8,128)(2,1)}, f32[2,512,256]{2,1,0:T(8,128)}, bf16[2,512,256]{2,1,0:T(8,128)(2,1)}, bf16[2,512,256]{2,1,0:T(8,128)(2,1)}) custom-call(f32[10]{0:T(128)} %add.160.counts_ref, bf16[512,768]{1,0:T(8,128)(2,1)} %bitcast.105, bf16[512,768]{1,0:T(8,128)(2,1)} %bitcast.98, ...), custom_call_target="tpu_custom_call" | custom-call | flops 2013265920 | bytes 5242880 | tf_op jit(solution)/shard_map/pallas_call | solution.py:134
  68.3 2.2 %collective-permute-start.13 = (bf16[2,512,256]{2,1,0:T(8,128)(2,1)}, bf16[2,512,256]{2,1,0:T(8,128)(2,1)}, u32[]{:S(2)}, u32[]{:S(2)}) collective-permute-start(bf16[2,512,256]{2,1,0:T(8,128)(2,1)} %get-tuple-element.29), channel_id=1, source_target_pairs={{0,24},{8,0},{16,8},{24,16},{1,25},{9,1},{17,9},{25,17},{2,26},{10... | collective-permute-start | bytes 1572872 | tf_op jit(solution)/shard_map/ppermute | solution.py:27
  70.5 10.7 %shard_map.103 = (bf16[512,256]{1,0:T(8,128)(2,1)}, bf16[512,256]{1,0:T(8,128)(2,1)}, f32[2,512,256]{2,1,0:T(8,128)}, bf16[2,512,256]{2,1,0:T(8,128)(2,1)}, bf16[2,512,256]{2,1,0:T(8,128)(2,1)}) custom-call(f32[10]{0:T(128)} %add.160.counts_ref, bf16[512,768]{1,0:T(8,128)(2,1)} %bitcast.106, bf16[512,768]{1,0:T(8,128)(2,1)} %bitcast.99, ...), custom_call_target="tpu_custom_call" | custom-call | flops 2013265920 | bytes 5242880 | tf_op jit(solution)/shard_map/pallas_call | solution.py:134
  81.2 3.9 %collective-permute-start.11 = (bf16[2,512,256]{2,1,0:T(8,128)(2,1)}, bf16[2,512,256]{2,1,0:T(8,128)(2,1)}, u32[]{:S(2)}, u32[]{:S(2)}) collective-permute-start(bf16[2,512,256]{2,1,0:T(8,128)(2,1)} %get-tuple-element.26), channel_id=1, source_target_pairs={{0,24},{8,0},{16,8},{24,16},{1,25},{9,1},{17,9},{25,17},{2,26},{10... | collective-permute-start | bytes 1572872 | tf_op jit(solution)/shard_map/ppermute | solution.py:27
  85.1 10.7 %shard_map.102 = (bf16[512,256]{1,0:T(8,128)(2,1)}, bf16[512,256]{1,0:T(8,128)(2,1)}, f32[2,512,256]{2,1,0:T(8,128)}, bf16[2,512,256]{2,1,0:T(8,128)(2,1)}, bf16[2,512,256]{2,1,0:T(8,128)(2,1)}) custom-call(f32[10]{0:T(128)} %add.160.counts_ref, bf16[512,768]{1,0:T(8,128)(2,1)} %bitcast.107, bf16[512,768]{1,0:T(8,128)(2,1)} %bitcast.100, ...), custom_call_target="tpu_custom_call" | custom-call | flops 2013265920 | bytes 5242880 | tf_op jit(solution)/shard_map/pallas_call | solution.py:134
  95.8 3.9 %collective-permute-start.9 = (bf16[2,512,256]{2,1,0:T(8,128)(2,1)}, bf16[2,512,256]{2,1,0:T(8,128)(2,1)S(1)}, u32[]{:S(2)}, u32[]{:S(2)}) collective-permute-start(bf16[2,512,256]{2,1,0:T(8,128)(2,1)} %get-tuple-element.23), channel_id=1, source_target_pairs={{0,24},{8,0},{16,8},{24,16},{1,25},{9,1},{17,9},{25,17},{2,26},{10... | collective-permute-start | bytes 1572872 | tf_op jit(solution)/shard_map/ppermute | solution.py:27
  108.8 5.2 %collective-permute-done.11 = bf16[2,512,256]{2,1,0:T(8,128)(2,1)} collective-permute-done((bf16[2,512,256]{2,1,0:T(8,128)(2,1)}, bf16[2,512,256]{2,1,0:T(8,128)(2,1)}, u32[]{:S(2)}, u32[]{:S(2)}) %collective-permute-start.11) | collective-permute-done | bytes 524320 | tf_op jit(solution)/shard_map/ppermute | solution.py:27
  115.5 9.7 %collective-permute-done.12 = bf16[2,512,256]{2,1,0:T(8,128)(2,1)} collective-permute-done((bf16[2,512,256]{2,1,0:T(8,128)(2,1)}, bf16[2,512,256]{2,1,0:T(8,128)(2,1)}, u32[]{:S(2)}, u32[]{:S(2)}) %collective-permute-start.12) | collective-permute-done | bytes 524320 | tf_op jit(solution)/shard_map/ppermute | solution.py:27
  128.1 8.0 %collective-permute-done.9 = bf16[2,512,256]{2,1,0:T(8,128)(2,1)S(1)} collective-permute-done((bf16[2,512,256]{2,1,0:T(8,128)(2,1)}, bf16[2,512,256]{2,1,0:T(8,128)(2,1)S(1)}, u32[]{:S(2)}, u32[]{:S(2)}) %collective-permute-start.9) | collective-permute-done | bytes 524320 | tf_op jit(solution)/shard_map/ppermute | solution.py:27
  136.1 10.7 %collective-permute-done.10 = bf16[2,512,256]{2,1,0:T(8,128)(2,1)S(1)} collective-permute-done((bf16[2,512,256]{2,1,0:T(8,128)(2,1)S(1)}, bf16[2,512,256]{2,1,0:T(8,128)(2,1)S(1)}, u32[]{:S(2)}, u32[]{:S(2)}) %collective-permute-start.10) | collective-permute-done | bytes 524320 | tf_op jit(solution)/shard_map/ppermute | solution.py:27
  151.0 4.4 %collective-permute-done.18 = bf16[4,1,384,256]{3,2,0,1:T(8,128)(2,1)S(1)} collective-permute-done((bf16[4,1,384,256]{3,2,0,1:T(8,128)(2,1)S(1)}, bf16[4,1,384,256]{3,2,0,1:T(8,128)(2,1)S(1)}, u32[]{:S(2)}, u32[]{:S(2)}) %collective-permute-start.18) | collective-permute-done | bytes 786464 | tf_op jit(solution)/shard_map/ppermute | solution.py:32
  156.3 4.4 %collective-permute-done.16 = bf16[2,1,384,256]{3,2,0,1:T(8,128)(2,1)S(1)} collective-permute-done((bf16[2,1,384,256]{3,2,0,1:T(8,128)(2,1)S(1)}, bf16[2,1,384,256]{3,2,0,1:T(8,128)(2,1)S(1)}, u32[]{:S(2)}, u32[]{:S(2)}) %collective-permute-start.16) | collective-permute-done | bytes 393248 | tf_op jit(solution)/shard_map/ppermute | solution.py:32
  161.4 11.9 %collective-permute-done.22 = bf16[2,1,384,256]{3,2,1,0:T(8,128)(2,1)S(1)} collective-permute-done((bf16[2,1,384,256]{3,2,1,0:T(8,128)(2,1)S(1)}, bf16[2,1,384,256]{3,2,1,0:T(8,128)(2,1)S(1)}, u32[]{:S(2)}, u32[]{:S(2)}) %collective-permute-start.22) | collective-permute-done | bytes 393248 | tf_op jit(solution)/shard_map/ppermute | solution.py:32
  173.6 8.5 %collective-permute-done.19 = bf16[2,1,384,256]{3,2,1,0:T(8,128)(2,1)S(1)} collective-permute-done((bf16[2,1,384,256]{3,2,1,0:T(8,128)(2,1)S(1)}, bf16[2,1,384,256]{3,2,1,0:T(8,128)(2,1)S(1)}, u32[]{:S(2)}, u32[]{:S(2)}) %collective-permute-start.19) | collective-permute-done | bytes 393248 | tf_op jit(solution)/shard_map/ppermute | solution.py:32
  182.3 10.2 %collective-permute-done.23 = bf16[1,1,384,256]{3,2,1,0:T(8,128)(2,1)S(1)} collective-permute-done((bf16[1,1,384,256]{3,2,1,0:T(8,128)(2,1)S(1)}, bf16[1,1,384,256]{3,2,1,0:T(8,128)(2,1)S(1)}, u32[]{:S(2)}, u32[]{:S(2)}) %collective-permute-start.23) | collective-permute-done | bytes 196640 | tf_op jit(solution)/shard_map/ppermute | solution.py:32
  192.6 2.1 %collective-permute-done.20 = bf16[1,1,384,256]{3,2,1,0:T(8,128)(2,1)S(1)} collective-permute-done((bf16[1,1,384,256]{3,2,1,0:T(8,128)(2,1)S(1)}, bf16[1,1,384,256]{3,2,1,0:T(8,128)(2,1)S(1)}, u32[]{:S(2)}, u32[]{:S(2)}) %collective-permute-start.20) | collective-permute-done | bytes 196640 | tf_op jit(solution)/shard_map/ppermute | solution.py:32
  (98 shorter events, 34.5 us)
Async XLA Ops:
  0.7 23.3 %collective-permute-start = (bf16[128,3072]{1,0:T(8,128)(2,1)}, bf16[128,3072]{1,0:T(8,128)(2,1)}, u32[]{:S(2)}, u32[]{:S(2)}) collective-permute-start(bf16[128,3072]{1,0:T(8,128)(2,1)} %bitcast.95), channel_id=1, source_target_pairs={{0,2},{2,0},{4,6},{6,4},{1,3},{3,1},{5,7},{7,5},{8,10},{10,8},{12,... | collective-permute-start | bytes 2359304 | tf_op jit(solution)/shard_map/ppermute | solution.py:32
  1.2 21.0 %collective-permute-start.1 = (bf16[128,3072]{1,0:T(8,128)(2,1)}, bf16[128,3072]{1,0:T(8,128)(2,1)}, u32[]{:S(2)}, u32[]{:S(2)}) collective-permute-start(bf16[128,3072]{1,0:T(8,128)(2,1)} %bitcast.96), channel_id=1, source_target_pairs={{0,4},{2,6},{4,0},{6,2},{1,5},{3,7},{5,1},{7,3},{8,12},{10,14},{12... | collective-permute-start | bytes 2359304 | tf_op jit(solution)/shard_map/ppermute | solution.py:32
  6.8 63.8 %collective-permute-start.6 = (bf16[2,512,256]{2,1,0:T(8,128)(2,1)}, bf16[2,512,256]{2,1,0:T(8,128)(2,1)}, u32[]{:S(2)}, u32[]{:S(2)}) collective-permute-start(bf16[2,512,256]{2,1,0:T(8,128)(2,1)} %pad_maximum_fusion.3), channel_id=1, source_target_pairs={{0,24},{8,0},{16,8},{24,16},{1,25},{9,1},{17,9},{25,17},{2,26},{10... | collective-permute-start | bytes 1572872 | tf_op jit(solution)/shard_map/ppermute | solution.py:27
  10.4 60.2 %collective-permute-start.5 = (bf16[2,512,256]{2,1,0:T(8,128)(2,1)}, bf16[2,512,256]{2,1,0:T(8,128)(2,1)}, u32[]{:S(2)}, u32[]{:S(2)}) collective-permute-start(bf16[2,512,256]{2,1,0:T(8,128)(2,1)} %pad_maximum_fusion.3), channel_id=1, source_target_pairs={{0,8},{8,16},{16,24},{24,0},{1,9},{9,17},{17,25},{25,1},{2,10},{10... | collective-permute-start | bytes 1572872 | tf_op jit(solution)/shard_map/ppermute | solution.py:27
  11.2 34.3 %collective-permute-start.8 = (bf16[2,512,256]{2,1,0:T(8,128)(2,1)}, bf16[2,512,256]{2,1,0:T(8,128)(2,1)}, u32[]{:S(2)}, u32[]{:S(2)}) collective-permute-start(bf16[2,512,256]{2,1,0:T(8,128)(2,1)} %pad_maximum_fusion.4), channel_id=1, source_target_pairs={{0,24},{8,0},{16,8},{24,16},{1,25},{9,1},{17,9},{25,17},{2,26},{10... | collective-permute-start | bytes 1572872 | tf_op jit(solution)/shard_map/ppermute | solution.py:27
  22.2 6.0 %collective-permute-start.2 = (bf16[128,3072]{1,0:T(8,128)(2,1)}, bf16[128,3072]{1,0:T(8,128)(2,1)S(1)}, u32[]{:S(2)}, u32[]{:S(2)}) collective-permute-start(bf16[128,3072]{1,0:T(8,128)(2,1)} %collective-permute-done.1), channel_id=1, source_target_pairs={{0,2},{2,0},{4,6},{6,4},{1,3},{3,1},{5,7},{7,5},{8,10},{10,8},{12,... | collective-permute-start | bytes 2359304 | tf_op jit(solution)/shard_map/ppermute | solution.py:32
  24.0 33.7 %collective-permute-start.7 = (bf16[2,512,256]{2,1,0:T(8,128)(2,1)}, bf16[2,512,256]{2,1,0:T(8,128)(2,1)}, u32[]{:S(2)}, u32[]{:S(2)}) collective-permute-start(bf16[2,512,256]{2,1,0:T(8,128)(2,1)} %pad_maximum_fusion.4), channel_id=1, source_target_pairs={{0,8},{8,16},{16,24},{24,0},{1,9},{9,17},{17,25},{25,1},{2,10},{10... | collective-permute-start | bytes 1572872 | tf_op jit(solution)/shard_map/ppermute | solution.py:27
  28.2 56.8 %collective-permute-start.4 = (bf16[2,512,256]{2,1,0:T(8,128)(2,1)}, bf16[2,512,256]{2,1,0:T(8,128)(2,1)}, u32[]{:S(2)}, u32[]{:S(2)}) collective-permute-start(bf16[2,512,256]{2,1,0:T(8,128)(2,1)} %pad_maximum_fusion.2), channel_id=1, source_target_pairs={{0,24},{8,0},{16,8},{24,16},{1,25},{9,1},{17,9},{25,17},{2,26},{10... | collective-permute-start | bytes 1572872 | tf_op jit(solution)/shard_map/ppermute | solution.py:27
  45.5 39.5 %collective-permute-start.3 = (bf16[2,512,256]{2,1,0:T(8,128)(2,1)}, bf16[2,512,256]{2,1,0:T(8,128)(2,1)}, u32[]{:S(2)}, u32[]{:S(2)}) collective-permute-start(bf16[2,512,256]{2,1,0:T(8,128)(2,1)} %pad_maximum_fusion.2), channel_id=1, source_target_pairs={{0,8},{8,16},{16,24},{24,0},{1,9},{9,17},{17,25},{25,1},{2,10},{10... | collective-permute-start | bytes 1572872 | tf_op jit(solution)/shard_map/ppermute | solution.py:27
  68.3 37.5 %collective-permute-start.13 = (bf16[2,512,256]{2,1,0:T(8,128)(2,1)}, bf16[2,512,256]{2,1,0:T(8,128)(2,1)}, u32[]{:S(2)}, u32[]{:S(2)}) collective-permute-start(bf16[2,512,256]{2,1,0:T(8,128)(2,1)} %get-tuple-element.29), channel_id=1, source_target_pairs={{0,24},{8,0},{16,8},{24,16},{1,25},{9,1},{17,9},{25,17},{2,26},{10... | collective-permute-start | bytes 1572872 | tf_op jit(solution)/shard_map/ppermute | solution.py:27
  70.5 35.3 %collective-permute-start.14 = (bf16[2,512,256]{2,1,0:T(8,128)(2,1)}, bf16[2,512,256]{2,1,0:T(8,128)(2,1)}, u32[]{:S(2)}, u32[]{:S(2)}) collective-permute-start(bf16[2,512,256]{2,1,0:T(8,128)(2,1)} %get-tuple-element.30), channel_id=1, source_target_pairs={{0,8},{8,16},{16,24},{24,0},{1,9},{9,17},{17,25},{25,1},{2,10},{10... | collective-permute-start | bytes 1572872 | tf_op jit(solution)/shard_map/ppermute | solution.py:27
  81.2 32.8 %collective-permute-start.11 = (bf16[2,512,256]{2,1,0:T(8,128)(2,1)}, bf16[2,512,256]{2,1,0:T(8,128)(2,1)}, u32[]{:S(2)}, u32[]{:S(2)}) collective-permute-start(bf16[2,512,256]{2,1,0:T(8,128)(2,1)} %get-tuple-element.26), channel_id=1, source_target_pairs={{0,24},{8,0},{16,8},{24,16},{1,25},{9,1},{17,9},{25,17},{2,26},{10... | collective-permute-start | bytes 1572872 | tf_op jit(solution)/shard_map/ppermute | solution.py:27
  85.1 40.2 %collective-permute-start.12 = (bf16[2,512,256]{2,1,0:T(8,128)(2,1)}, bf16[2,512,256]{2,1,0:T(8,128)(2,1)}, u32[]{:S(2)}, u32[]{:S(2)}) collective-permute-start(bf16[2,512,256]{2,1,0:T(8,128)(2,1)} %get-tuple-element.27), channel_id=1, source_target_pairs={{0,8},{8,16},{16,24},{24,0},{1,9},{9,17},{17,25},{25,1},{2,10},{10... | collective-permute-start | bytes 1572872 | tf_op jit(solution)/shard_map/ppermute | solution.py:27
  95.8 40.3 %collective-permute-start.9 = (bf16[2,512,256]{2,1,0:T(8,128)(2,1)}, bf16[2,512,256]{2,1,0:T(8,128)(2,1)S(1)}, u32[]{:S(2)}, u32[]{:S(2)}) collective-permute-start(bf16[2,512,256]{2,1,0:T(8,128)(2,1)} %get-tuple-element.23), channel_id=1, source_target_pairs={{0,24},{8,0},{16,8},{24,16},{1,25},{9,1},{17,9},{25,17},{2,26},{10... | collective-permute-start | bytes 1572872 | tf_op jit(solution)/shard_map/ppermute | solution.py:27
  105.8 41.0 %collective-permute-start.10 = (bf16[2,512,256]{2,1,0:T(8,128)(2,1)S(1)}, bf16[2,512,256]{2,1,0:T(8,128)(2,1)S(1)}, u32[]{:S(2)}, u32[]{:S(2)}) collective-permute-start(bf16[2,512,256]{2,1,0:T(8,128)(2,1)S(1)} %copy-done.11), channel_id=1, source_target_pairs={{0,8},{8,16},{16,24},{24,0},{1,9},{9,17},{17,25},{25,1},{2,10},{10... | collective-permute-start | bytes 1572872 | tf_op jit(solution)/shard_map/ppermute | solution.py:27
  105.8 42.5 %collective-permute-start.15 = (bf16[4,1,384,256]{3,2,0,1:T(8,128)(2,1)S(1)}, bf16[4,1,384,256]{3,2,0,1:T(8,128)(2,1)S(1)}, u32[]{:S(2)}, u32[]{:S(2)}) collective-permute-start(bf16[4,1,384,256]{3,2,0,1:T(8,128)(2,1)S(1)} %fusion.2), channel_id=1, source_target_pairs={{0,1},{1,0},{2,3},{3,2},{4,5},{5,4},{6,7},{7,6},{8,9},{9,8},{10,11... | collective-permute-start | bytes 2359304 | tf_op jit(solution)/shard_map/ppermute | solution.py:32
  114.0 36.3 %collective-permute-start.21 = (bf16[4,1,384,256]{3,2,0,1:T(8,128)(2,1)S(1)}, bf16[4,1,384,256]{3,2,0,1:T(8,128)(2,1)S(1)}, u32[]{:S(2)}, u32[]{:S(2)}) collective-permute-start(bf16[4,1,384,256]{3,2,0,1:T(8,128)(2,1)S(1)} %fusion.1), channel_id=1, source_target_pairs={{0,1},{1,0},{2,3},{3,2},{4,5},{5,4},{6,7},{7,6},{8,9},{9,8},{10,11... | collective-permute-start | bytes 2359304 | tf_op jit(solution)/shard_map/ppermute | solution.py:32
  125.2 30.2 %collective-permute-start.18 = (bf16[4,1,384,256]{3,2,0,1:T(8,128)(2,1)S(1)}, bf16[4,1,384,256]{3,2,0,1:T(8,128)(2,1)S(1)}, u32[]{:S(2)}, u32[]{:S(2)}) collective-permute-start(bf16[4,1,384,256]{3,2,0,1:T(8,128)(2,1)S(1)} %fusion), channel_id=1, source_target_pairs={{0,1},{1,0},{2,3},{3,2},{4,5},{5,4},{6,7},{7,6},{8,9},{9,8},{10,11... | collective-permute-start | bytes 2359304 | tf_op jit(solution)/shard_map/ppermute | solution.py:32
  148.6 12.1 %collective-permute-start.16 = (bf16[2,1,384,256]{3,2,0,1:T(8,128)(2,1)S(1)}, bf16[2,1,384,256]{3,2,0,1:T(8,128)(2,1)S(1)}, u32[]{:S(2)}, u32[]{:S(2)}) collective-permute-start(bf16[2,1,384,256]{3,2,0,1:T(8,128)(2,1)S(1)} %fusion.3), channel_id=1, source_target_pairs={{0,8},{8,0},{16,24},{24,16},{1,9},{9,1},{17,25},{25,17},{2,10},{10... | collective-permute-start | bytes 1179656 | tf_op jit(solution)/shard_map/ppermute | solution.py:32
  150.5 22.8 %collective-permute-start.22 = (bf16[2,1,384,256]{3,2,1,0:T(8,128)(2,1)S(1)}, bf16[2,1,384,256]{3,2,1,0:T(8,128)(2,1)S(1)}, u32[]{:S(2)}, u32[]{:S(2)}) collective-permute-start(bf16[2,1,384,256]{3,2,1,0:T(8,128)(2,1)S(1)} %fusion.5), channel_id=1, source_target_pairs={{0,8},{8,0},{16,24},{24,16},{1,9},{9,1},{17,25},{25,17},{2,10},{10... | collective-permute-start | bytes 1179656 | tf_op jit(solution)/shard_map/ppermute | solution.py:32
  155.6 26.5 %collective-permute-start.19 = (bf16[2,1,384,256]{3,2,1,0:T(8,128)(2,1)S(1)}, bf16[2,1,384,256]{3,2,1,0:T(8,128)(2,1)S(1)}, u32[]{:S(2)}, u32[]{:S(2)}) collective-permute-start(bf16[2,1,384,256]{3,2,1,0:T(8,128)(2,1)S(1)} %fusion.4), channel_id=1, source_target_pairs={{0,8},{8,0},{16,24},{24,16},{1,9},{9,1},{17,25},{25,17},{2,10},{10... | collective-permute-start | bytes 1179656 | tf_op jit(solution)/shard_map/ppermute | solution.py:32
  160.8 21.4 %collective-permute-start.17 = (bf16[1,1,384,256]{3,2,0,1:T(8,128)(2,1)S(1)}, bf16[1,1,384,256]{3,2,0,1:T(8,128)(2,1)S(1)}, u32[]{:S(2)}, u32[]{:S(2)}) collective-permute-start(bf16[1,1,384,256]{3,2,0,1:T(8,128)(2,1)S(1)} %dynamic-slice_convert_fusion.3), channel_id=1, source_target_pairs={{0,16},{8,24},{16,0},{24,8},{1,17},{9,25},{17,1},{25,9},{2,18},{10... | collective-permute-start | bytes 589832 | tf_op jit(solution)/shard_map/ppermute | solution.py:32
  173.5 19.0 %collective-permute-start.23 = (bf16[1,1,384,256]{3,2,1,0:T(8,128)(2,1)S(1)}, bf16[1,1,384,256]{3,2,1,0:T(8,128)(2,1)S(1)}, u32[]{:S(2)}, u32[]{:S(2)}) collective-permute-start(bf16[1,1,384,256]{3,2,1,0:T(8,128)(2,1)S(1)} %dynamic-slice_convert_fusion.1), channel_id=1, source_target_pairs={{0,16},{8,24},{16,0},{24,8},{1,17},{9,25},{17,1},{25,9},{2,18},{10... | collective-permute-start | bytes 589832 | tf_op jit(solution)/shard_map/ppermute | solution.py:32
  182.2 12.5 %collective-permute-start.20 = (bf16[1,1,384,256]{3,2,1,0:T(8,128)(2,1)S(1)}, bf16[1,1,384,256]{3,2,1,0:T(8,128)(2,1)S(1)}, u32[]{:S(2)}, u32[]{:S(2)}) collective-permute-start(bf16[1,1,384,256]{3,2,1,0:T(8,128)(2,1)S(1)} %dynamic-slice_convert_fusion.2), channel_id=1, source_target_pairs={{0,16},{8,24},{16,0},{24,8},{1,17},{9,25},{17,1},{25,9},{2,18},{10... | collective-permute-start | bytes 589832 | tf_op jit(solution)/shard_map/ppermute | solution.py:32
  (12 other events, 134.0 us)

commit v2 on v0

v2 whole, which is shorter than its diff:
```python
import functools
import math

import jax
import jax.numpy as jnp
from jax import lax
from jax.experimental import pallas as pl
from jax.experimental.pallas import tpu as pltpu
from jax.sharding import PartitionSpec as P

HEAD_DIM = 128
TILE = 256
REACH = 2
WIDE = 2 * REACH + 1
CHUNK_HEADS = 2
BLOCK = 256
NT = (((1,), (1,)), ((), ()))
NN = (((1,), (0,)), ((), ()))
TN = (((0,), (0,)), ((), ()))
MESH = pl.DeviceIdType.MESH


def mul(a, b, dims):
    return lax.dot_general(a, b, dims, preferred_element_type=jnp.float32)


def columns(start, size):
    return pl.ds(pl.multiple_of(start, HEAD_DIM), size)


def attend_head(col, att_col, counts_ref, refs):
    factor = 1.0 / math.sqrt(HEAD_DIM)
    q_s, k_s, v_s, ga, kv_in, dq_ref, att_s, own, dsend, ext = refs
    rows = q_s.shape[0]
    tiles = rows // TILE
    lanes = columns(col, HEAD_DIM)

    def tile_of(n, j):
        part, at = divmod(j, tiles)
        here = slice(at * TILE, (at + 1) * TILE)
        if part == 1:
            return (k_s, v_s)[n][here, lanes]
        return kv_in[part // 2, n, here, lanes]

    seen = set()
    for i in range(tiles):
        here = slice(i * TILE, (i + 1) * TILE)
        q = q_s[here, lanes]
        g = ga[here, lanes]
        spots = [i + tiles - REACH + o for o in range(WIDE)]
        live = [counts_ref[i * WIDE + o] for o in range(WIDE)]
        scores = []
        top = None
        for o in range(WIDE):
            bias = jnp.where(live[o] > 0.0, 0.0, -jnp.inf)
            s = mul(tile_of(0, spots[o]), q, NT) * factor + bias
            scores.append(s)
            m = jnp.max(s, axis=0, keepdims=True)
            top = m if top is None else jnp.maximum(top, m)
        total = None
        raised = []
        for o in range(WIDE):
            e = jnp.exp(scores[o] - top)
            raised.append(e)
            part = jnp.sum(e, axis=0, keepdims=True) * live[o]
            total = part if total is None else total + part
        inverse = 1.0 / total
        weights = []
        att = None
        for o in range(WIDE):
            w = raised[o] * inverse
            weights.append(w)
            low = w.astype(jnp.bfloat16)
            part = mul(tile_of(1, spots[o]), low, TN) * live[o]
            att = part if att is None else att + part
            dv = mul(low, g, NN) * live[o]
            spot = slice(spots[o] * TILE, (spots[o] + 1) * TILE)
            if spots[o] in seen:
                ext[1, spot] += dv
            else:
                ext[1, spot] = dv
        att_s[here, columns(att_col, HEAD_DIM)] = att.T.astype(jnp.bfloat16)
        g_turned = g.astype(jnp.float32).T
        delta = jnp.sum(
            g_turned * att.astype(jnp.bfloat16).astype(jnp.float32), axis=0, keepdims=True
        )
        dq = None
        for o in range(WIDE):
            dw = mul(tile_of(1, spots[o]), g, NT)
            ds = (weights[o] * (dw - delta) * factor).astype(jnp.bfloat16)
            part = mul(tile_of(0, spots[o]), ds, TN) * live[o]
            dq = part if dq is None else dq + part
            dk = mul(ds, q, NN) * live[o]
            spot = slice(spots[o] * TILE, (spots[o] + 1) * TILE)
            if spots[o] in seen:
                ext[0, spot] += dk
            else:
                ext[0, spot] = dk
            seen.add(spots[o])
        dq_ref[here, lanes] = dq.T.astype(jnp.bfloat16)
    for n in range(2):
        dsend[0, n, :, lanes] = ext[n, 0:rows].astype(jnp.bfloat16)
        own[n, :, lanes] = ext[n, rows : 2 * rows]
        dsend[1, n, :, lanes] = ext[n, 2 * rows : 3 * rows].astype(jnp.bfloat16)


def kernel(
    sizes,
    counts_ref,
    q_ref,
    k_ref,
    v_ref,
    og_ref,
    w_ref,
    dq_ref,
    dk_ref,
    dv_ref,
    gw_ref,
    q_s,
    k_s,
    v_s,
    w_s,
    og_s,
    og_t,
    ga,
    kv_in,
    ext,
    own,
    dsend,
    drecv,
    att_s,
    gw_s,
    acc,
    wsend,
    wrecv,
    local_sem,
    kv_ss,
    kv_rs,
    og_ss,
    og_rs,
    d_ss,
    d_rs,
    w_ss,
    w_rs,
):
    lon_count, head_count, dp_count = sizes
    rows, features = q_s.shape
    model = og_s.shape[1]
    piece = og_ref.shape[0]
    cols = CHUNK_HEADS * HEAD_DIM
    chunks = features // cols
    lon = lax.axis_index("lon")
    head = lax.axis_index("head")
    dp = lax.axis_index("dp")
    after = {"lon": lax.rem(lon + 1, lon_count)}
    before = {"lon": lax.rem(lon + lon_count - 1, lon_count)}

    def partner(axis, me, bit):
        low = lax.rem(me // bit, 2)
        return {axis: me + bit - 2 * bit * low}, low

    stages = []
    for axis, me, count in (("dp", dp, dp_count), ("lon", lon, lon_count)):
        bit = 1
        while bit < count:
            stages.append(partner(axis, me, bit))
            bit *= 2
    gathers = []
    held = [0]
    bit = head_count // 2
    while bit:
        for at in list(held):
            gathers.append((bit, at))
            held.append(at + bit)
        bit //= 2

    greeted = [after, before] + [there for there, _ in stages]
    bit = head_count // 2
    while bit:
        greeted.append(partner("head", head, bit)[0])
        bit //= 2
    barrier = pltpu.get_barrier_semaphore()
    for there in greeted:
        pl.semaphore_signal(barrier, inc=1, device_id=there, device_id_type=MESH)
    pl.semaphore_wait(barrier, len(greeted))

    def remote(src, dst, ss, rs, there):
        return pltpu.make_async_remote_copy(
            src_ref=src, dst_ref=dst, send_sem=ss, recv_sem=rs, device_id=there, device_id_type=MESH
        )

    def piece_at(offset):
        at = 0
        bit = 1
        while bit < head_count:
            low = lax.rem(head // bit, 2)
            at = at + bit * ((1 - low) if offset & bit else low)
            bit *= 2
        return pl.ds(pl.multiple_of(at * piece, piece), piece)

    kv_copies = []
    d_copies = []
    for c in range(chunks):
        cut = slice(c * cols, (c + 1) * cols)
        some, others = [], []
        for n, ref in ((0, k_ref), (1, v_ref)):
            for way, there in ((0, after), (1, before)):
                at = (c * 2 + n) * 2 + way
                some.append(
                    remote(
                        ref.at[:, cut], kv_in.at[way, n, :, cut], kv_ss.at[at], kv_rs.at[at], there
                    )
                )
            for way, there in ((0, before), (1, after)):
                at = (c * 2 + n) * 2 + way
                others.append(
                    remote(
                        dsend.at[way, n, :, cut],
                        drecv.at[way, n, :, cut],
                        d_ss.at[at],
                        d_rs.at[at],
                        there,
                    )
                )
        kv_copies.append(some)
        d_copies.append(others)

    og_copies = []
    for at, (bit, offset) in enumerate(gathers):
        src = og_ref if offset == 0 else og_s.at[piece_at(offset)]
        og_copies.append(
            remote(
                src,
                og_s.at[piece_at(offset)],
                og_ss.at[at],
                og_rs.at[at],
                partner("head", head, bit)[0],
            )
        )
    for copy in kv_copies[0]:
        copy.start()
    for copy, (bit, offset) in zip(og_copies, gathers):
        if offset == 0:
            copy.start()
    for some in kv_copies[1:]:
        for copy in some:
            copy.start()
    local_copies = [
        pltpu.make_async_copy(src, dst, local_sem.at[at])
        for at, (src, dst) in enumerate(
            (
                (og_ref, og_s.at[piece_at(0)]),
                (w_ref, w_s),
                (q_ref, q_s),
                (k_ref, k_s),
                (v_ref, v_s),
            )
        )
    ]
    for copy in local_copies:
        copy.start()
    where = {}
    for at, (bit, offset) in enumerate(gathers):
        where[bit + offset] = at
    arrived = set()
    for copy, (bit, offset) in zip(og_copies, gathers):
        if offset:
            og_copies[where[offset]].wait_recv()
            arrived.add(where[offset])
            copy.start()
    for at, copy in enumerate(og_copies):
        if at not in arrived:
            copy.wait_recv()
    for copy in local_copies:
        copy.wait()

    @pl.loop(0, chunks)
    def _(c):
        ga[:, columns(c * cols, cols)] = mul(
            og_s[...], w_s[pl.ds(pl.multiple_of(c * cols, cols), cols)], NT
        ).astype(jnp.bfloat16)

    @pl.loop(0, model // BLOCK)
    def _(b):
        og_t[pl.ds(pl.multiple_of(b * BLOCK, BLOCK), BLOCK)] = og_s[:, columns(b * BLOCK, BLOCK)].T

    shares = lon_count * dp_count
    share = model // shares
    last = len(stages)
    sent_counts = [shares >> (s + 1) for s in range(last)]
    starts = [sum(sent_counts[:s]) for s in range(last)]

    def weight_copy(s, c):
        span = pl.ds(starts[s], sent_counts[s])
        at = c * last + s
        return remote(
            wsend.at[c, span], wrecv.at[c, span], w_ss.at[at], w_rs.at[at], stages[s][0]
        )

    def share_rows(b):
        return pl.ds(pl.multiple_of(b * share, 16), share)

    def stage(s, c):
        if s > 0:
            weight_copy(s - 1, c).wait_recv()

            @pl.loop(0, sent_counts[s - 1])
            def _(j):
                acc[c, j] += wrecv[c, starts[s - 1] + j].astype(jnp.float32)

        if s == last:
            gw_ref[:, c * cols : (c + 1) * cols] = acc[c, 0]
            return
        mine = stages[s][1]

        @pl.loop(0, sent_counts[s])
        def _(j):
            if s == 0:
                gone = gw_s[share_rows(2 * j + 1 - mine)]
                kept = gw_s[share_rows(2 * j + mine)]
            else:
                gone = acc[c, 2 * j + 1 - mine]
                kept = acc[c, 2 * j + mine]
            wsend[c, starts[s] + j] = gone.astype(jnp.bfloat16)
            acc[c, j] = kept

        weight_copy(s, c).start()

    refs = (q_s, k_s, v_s, ga, kv_in, dq_ref, att_s, own, dsend, ext)
    for c in range(chunks):
        for copy in kv_copies[c]:
            copy.wait_recv()

        @pl.loop(0, CHUNK_HEADS)
        def _(h):
            attend_head(c * cols + h * HEAD_DIM, h * HEAD_DIM, counts_ref, refs)

        for copy in d_copies[c]:
            copy.start()

        @pl.loop(0, model // BLOCK)
        def _(b):
            span = pl.ds(pl.multiple_of(b * BLOCK, BLOCK), BLOCK)
            gw_s[span] = mul(og_t[span], att_s[...], NN)

        stage(0, c)
        if c > 0:
            stage(1, c - 1)
    stage(1, chunks - 1)
    for s in range(2, last + 1):
        for c in range(chunks):
            if s == 2:
                cut = slice(c * cols, (c + 1) * cols)
                for copy in d_copies[c]:
                    copy.wait_recv()
                for n, ref in ((0, dk_ref), (1, dv_ref)):
                    ref[:, cut] = (
                        own[n, :, cut]
                        + drecv[0, n, :, cut].astype(jnp.float32)
                        + drecv[1, n, :, cut].astype(jnp.float32)
                    ).astype(jnp.bfloat16)
            stage(s, c)
    for copy in og_copies:
        copy.wait_send()
    for c in range(chunks):
        for copy in kv_copies[c] + d_copies[c]:
            copy.wait_send()
        for s in range(last):
            weight_copy(s, c).wait_send()


def local(queries, key_heads, value_heads, out_grad, out_weight, neighbours, slot_valid):
    q, k, v = queries[0], key_heads[0], value_heads[0]
    rows, features = q.shape
    tiles = rows // TILE
    sizes = tuple(lax.axis_size(axis) for axis in ("lon", "head", "dp"))
    lon_count, head_count, dp_count = sizes
    tile_total = tiles * lon_count
    first_tile = lax.axis_index("lon") * tiles
    own_rows = lax.dynamic_slice_in_dim(neighbours, first_tile, tiles, 0)
    own_live = lax.dynamic_slice_in_dim(slot_valid, first_tile, tiles, 0)
    index = first_tile + jnp.arange(tiles, dtype=jnp.int32)
    offset = (own_rows - index[:, None] + REACH + tile_total) % tile_total
    span = jnp.arange(WIDE, dtype=jnp.int32)
    named = (offset[:, :, None] == span) & (own_live > 0)[:, :, None]
    counts = jnp.sum(named.astype(jnp.float32), axis=1) + (span == REACH).astype(jnp.float32)
    counts = counts.reshape(-1)

    model = out_weight.shape[1]
    cols = CHUNK_HEADS * HEAD_DIM
    chunks = features // cols
    shares = lon_count * dp_count
    share = model // shares
    bits = shares.bit_length() - 1
    low, wide = jnp.bfloat16, jnp.float32
    vmem = pltpu.VMEM
    dma = pltpu.SemaphoreType.DMA
    dq, dk, dv, gw = pl.pallas_call(
        functools.partial(kernel, sizes),
        out_shape=[
            jax.ShapeDtypeStruct((rows, features), low),
            jax.ShapeDtypeStruct((rows, features), low),
            jax.ShapeDtypeStruct((rows, features), low),
            jax.ShapeDtypeStruct((share, features), wide),
        ],
        in_specs=[pl.BlockSpec(memory_space=pltpu.SMEM)]
        + [pl.BlockSpec(memory_space=pl.ANY)] * 5,
        out_specs=[pl.BlockSpec(memory_space=vmem)] * 4,
        scratch_shapes=[
            vmem((rows, features), low),
            vmem((rows, features), low),
            vmem((rows, features), low),
            vmem((features, model), low),
            vmem((rows, model), low),
            vmem((model, rows), low),
            vmem((rows, features), low),
            vmem((2, 2, rows, features), low),
            vmem((2, 3 * rows, HEAD_DIM), wide),
            vmem((2, rows, features), wide),
            vmem((2, 2, rows, features), low),
            vmem((2, 2, rows, features), low),
            vmem((rows, cols), low),
            vmem((model, cols), wide),
            vmem((chunks, shares // 2, share, cols), wide),
            vmem((chunks, shares - 1, share, cols), low),
            vmem((chunks, shares - 1, share, cols), low),
            dma((5,)),
            dma((chunks * 4,)),
            dma((chunks * 4,)),
            dma((head_count - 1,)),
            dma((head_count - 1,)),
            dma((chunks * 4,)),
            dma((chunks * 4,)),
            dma((chunks * bits,)),
            dma((chunks * bits,)),
        ],
        compiler_params=pltpu.CompilerParams(
            collective_id=0, has_side_effects=True, vmem_limit_bytes=60 * 1024 * 1024
        ),
    )(counts, q, k, v, out_grad[0], out_weight)
    return (dq[None], dk[None], dv[None], gw)


def solution(mesh):
    in_specs = (
        P("dp", "lon", "head"),
        P("dp", "lon", "head"),
        P("dp", "lon", "head"),
        P("dp", ("lon", "head"), None),
        P("head", None),
        P(),
        P(),
    )
    out_specs = (
        P("dp", "lon", "head"),
        P("dp", "lon", "head"),
        P("dp", "lon", "head"),
        P(("lon", "dp"), "head"),
    )
    return jax.shard_map(local, mesh=mesh, in_specs=in_specs, out_specs=out_specs, check_vma=False)
```

time: 497 us -> 197 us (0.40)
  waiting for transfers between devices: 279 us -> 0 us
  Pallas kernels: 0 us -> 188 us
  local copies, waits for them, and re-layouts: 111 us -> 6.92 us
  matrix products: 52.1 us -> 0 us
  other arithmetic: 30.3 us -> 1.63 us
  between operations: 14.2 us -> 0.67 us
  starting transfers between devices: 7.21 us -> 0 us
    ppermute x4 -> x0, waiting for transfers between devices: 254 us -> none  [passed_along(): return lax.ppermute(value, axis, pairs)]
    pallas_call x0 -> x1, Pallas kernels: none -> 188 us  [local(): pl.pallas_call(functools.partial(kernel, sizes), out_shape=[jax.ShapeDtyp...]
    dot_general x38 -> x0, matrix products: 52.1 us -> none  [the longest x6 14.4 us: attend_head(): jnp.einsum('qisj,qsjd->qid', grad_scores, picked_keys, preferred_element_...]
    another operation x19 -> x0, local copies, waits for them, and re-layouts: 25.5 us -> none  [the longest x3 14.2 us: local(): jnp.stack((tokens_first(key_sums, 3 * token_count), tokens_first(value_su...]
    reduce_scatter x1 -> x0, waiting for transfers between devices: 25.1 us -> none  [local(): lax.psum_scatter(lax.dot_general(grad_rows, attn_out, (((0,), (0,)), ((),...]
    scatter-add x12 -> x0, other arithmetic: 19.9 us -> none  [the longest x6 9.93 us: attend_head(): jnp.zeros(value_tiles.shape, jnp.float32).at[slot_tiles].add(value_blocks)]
    transpose x3 -> x0, local copies, waits for them, and re-layouts: 17.9 us -> none  [tokens_first(): return blocks.transpose(1, 2, 0, 3).reshape(row_count, feature_count)]
    dynamic_slice x19 -> x0, local copies, waits for them, and re-layouts: 12.9 us -> none  [the longest x18 12.8 us: local(): lax.map(per_head, (heads_first(queries[0], token_count), heads_first(exte...]
  transfers between devices with their start and end apart: 6 -> 0, of which waited for: 5 -> 0; matrix products, arithmetic and copies ran while one was open for 13% -> 0% of each run, Pallas kernels for 0% -> 0%
where the time goes in v2:
time: 197 us
  Pallas kernels  188 us (95%)
  local copies, waits for them, and re-layouts  6.92 us (4%)
    pallas_call x1, Pallas kernels, local(): pl.pallas_call(functools.partial(kernel, sizes), out_shape=[jax.ShapeDtyp...  188 us
    unnamed x10, local copies, waits for them, and re-layouts  6.12 us

profile of v2, /device:TPU:0, one launch (start us, length us, event | category | flops | bytes accessed | tf_op | source)
XLA Modules:
  0.0 196.9 jit_solution(1628664555934148691)
XLA Ops:
  0.6 0.8 dynamic-slice_compare_fusion
  1.4 0.1 copy.14
  1.5 0.8 add_select_fusion
  2.3 0.1 copy.13
  2.4 0.1 convert_reduce_fusion
  2.5 0.6 add.48.counts_ref
  3.1 187.7 %shard_map.102 = (bf16[512,768]{1,0:T(8,128)(2,1)}, bf16[512,768]{1,0:T(8,128)(2,1)}, bf16[512,768]{1,0:T(8,128)(2,1)}, f32[384,768]{1,0:T(8,128)}) custom-call(f32[10]{0:T(128)} %add.48.counts_ref, bf16[512,768]{1,0:T(8,128)(2,1)} %bitcast.10, bf16[512,768]{1,0:T(8,128)(2,1)} %bitcast.11, bf16[512,768]{1,0:T(8,128)(2,1)} %bitcast.12, ...), custom_call_target="tpu_custom_call" | custom-call | tf_op jit(solution)/shard_map/pallas_call | solution.py:398
  190.7 0.0 copy-start.2
  190.8 2.1 %copy.19 = bf16[1,512,768]{2,1,0:T(8,128)(2,1)} copy(bf16[1,512,768]{2,1,0:T(8,128)(2,1)} %bitcast.9) | data formatting | bytes 1572864
  192.9 0.0 copy-done.2
  192.9 0.0 copy-start.1
  192.9 0.9 copy.20
  193.8 0.5 copy-done.1
  194.3 0.0 copy-start
  194.3 0.9 copy.21
  195.2 0.7 copy-done
  195.9 1.0 copy.22
  (3 shorter events, 0.0 us)
Async XLA Ops:
  190.7 2.1 %copy-start.2 = (bf16[512,768]{1,0:T(8,128)(2,1)S(1)}, bf16[512,768]{1,0:T(8,128)(2,1)}, u32[]{:S(2)}) copy-start(bf16[512,768]{1,0:T(8,128)(2,1)} %get-tuple-element.9) | copy-start | bytes 2359300
  192.9 1.4 copy-start.1
  194.3 1.6 copy-start

commit v3 on v2

--- a/solution.py
+++ b/solution.py
@@ -28,7 +28,7 @@
     return pl.ds(pl.multiple_of(start, HEAD_DIM), size)
 
 
-def attend_head(col, att_col, counts_ref, refs):
+def attend_head(col, att_col, counts, refs):
     factor = 1.0 / math.sqrt(HEAD_DIM)
     q_s, k_s, v_s, ga, kv_in, dq_ref, att_s, own, dsend, ext = refs
     rows = q_s.shape[0]
@@ -48,7 +48,7 @@
         q = q_s[here, lanes]
         g = ga[here, lanes]
         spots = [i + tiles - REACH + o for o in range(WIDE)]
-        live = [counts_ref[i * WIDE + o] for o in range(WIDE)]
+        live = counts[i]
         scores = []
         top = None
         for o in range(WIDE):
@@ -106,7 +106,8 @@
 
 def kernel(
     sizes,
-    counts_ref,
+    near_ref,
+    valid_ref,
     q_ref,
     k_ref,
     v_ref,
@@ -142,6 +143,11 @@
     d_rs,
     w_ss,
     w_rs,
+    relay_ss,
+    lsend,
+    lrecv,
+    l_ss,
+    l_rs,
 ):
     lon_count, head_count, dp_count = sizes
     rows, features = q_s.shape
@@ -152,6 +158,17 @@
     lon = lax.axis_index("lon")
     head = lax.axis_index("head")
     dp = lax.axis_index("dp")
+    line = lon_count == 4
+    tiles = rows // TILE
+    counts = []
+    for i in range(tiles):
+        tile = lon * tiles + i
+        live = [jnp.float32(1.0 if o == REACH else 0.0) for o in range(WIDE)]
+        for j in range(near_ref.shape[1]):
+            away = lax.rem(near_ref[tile, j] - tile + REACH + tiles * lon_count, tiles * lon_count)
+            used = jnp.where(valid_ref[tile, j] > 0, 1.0, 0.0)
+            live = [live[o] + jnp.where(away == o, used, 0.0) for o in range(WIDE)]
+        counts.append(live)
     after = {"lon": lax.rem(lon + 1, lon_count)}
     before = {"lon": lax.rem(lon + lon_count - 1, lon_count)}
 
@@ -160,7 +177,7 @@
         return {axis: me + bit - 2 * bit * low}, low
 
     stages = []
-    for axis, me, count in (("dp", dp, dp_count), ("lon", lon, lon_count)):
+    for axis, me, count in (("dp", dp, dp_count), ("lon", lon, 1 if line else lon_count)):
         bit = 1
         while bit < count:
             stages.append(partner(axis, me, bit))
@@ -175,6 +192,9 @@
         bit //= 2
 
     greeted = [after, before] + [there for there, _ in stages]
+    across = partner("lon", lon, 2)[0]
+    if line:
+        greeted.append(across)
     bit = head_count // 2
     while bit:
         greeted.append(partner("head", head, bit)[0])
@@ -237,14 +257,48 @@
                 partner("head", head, bit)[0],
             )
         )
-    for copy in kv_copies[0]:
-        copy.start()
+
+    def each_kv(c, act):
+        for at, copy in enumerate(kv_copies[c]):
+            if line:
+                pl.when(lon != (3 if at % 2 == 0 else 0))(functools.partial(act, copy))
+            else:
+                act(copy)
+
+    def relay(c, n, way):
+        cut = slice(c * cols, (c + 1) * cols)
+        return remote(
+            kv_in.at[way, n, :, cut],
+            kv_in.at[1 - way, n, :, cut],
+            relay_ss.at[c * 2 + n],
+            kv_rs.at[(c * 2 + n) * 2 + 1 - way],
+            across,
+        )
+
+    def pass_on(c):
+        if not line:
+            return
+        for way in range(2):
+
+            @pl.when(lon == 1 + way)
+            def _():
+                for n in range(2):
+                    kv_copies[c][n * 2 + way].wait_recv()
+                    relay(c, n, way).start()
+
+    def take(c):
+        for at, copy in enumerate(kv_copies[c]):
+            if line:
+                pl.when(lon != 1 + at % 2)(copy.wait_recv)
+            else:
+                copy.wait_recv()
+
+    each_kv(0, lambda copy: copy.start())
     for copy, (bit, offset) in zip(og_copies, gathers):
         if offset == 0:
             copy.start()
-    for some in kv_copies[1:]:
-        for copy in some:
-            copy.start()
+    for c in range(1, chunks - 1):
+        each_kv(c, lambda copy: copy.start())
     local_copies = [
         pltpu.make_async_copy(src, dst, local_sem.at[at])
         for at, (src, dst) in enumerate(
@@ -268,6 +322,8 @@
             og_copies[where[offset]].wait_recv()
             arrived.add(where[offset])
             copy.start()
+    pass_on(0)
+    each_kv(chunks - 1, lambda copy: copy.start())
     for at, copy in enumerate(og_copies):
         if at not in arrived:
             copy.wait_recv()
@@ -308,8 +364,10 @@
             def _(j):
                 acc[c, j] += wrecv[c, starts[s - 1] + j].astype(jnp.float32)
 
+        if s == last and not line:
+            gw_ref[:, c * cols : (c + 1) * cols] = acc[c, 0]
+            return
         if s == last:
-            gw_ref[:, c * cols : (c + 1) * cols] = acc[c, 0]
             return
         mine = stages[s][1]
 
@@ -326,14 +384,80 @@
 
         weight_copy(s, c).start()
 
+    def link(c, t, side):
+        at = c * 4 + t
+        return remote(
+            lsend.at[c, t],
+            lrecv.at[c, side, t],
+            l_ss.at[at],
+            l_rs.at[(c * 2 + side) * 4 + t],
+            before if side else after,
+        )
+
+    def hop(c, t, side, add):
+        total = acc[c, t]
+        if add:
+            link(c, t, side).wait_recv()
+            total = total + lrecv[c, side, t].astype(jnp.float32)
+        lsend[c, t] = total.astype(jnp.bfloat16)
+        link(c, t, side).start()
+
+    def chain(step, c):
+        if step == 0:
+
+            @pl.when(lon == 0)
+            def _():
+                for t in (3, 2, 1):
+                    hop(c, t, 0, False)
+
+            @pl.when(lon == 3)
+            def _():
+                for t in (0, 1, 2):
+                    hop(c, t, 1, False)
+
+        elif step == 1:
+
+            @pl.when(lon == 1)
+            def _():
+                for t in (3, 2):
+                    hop(c, t, 0, True)
+
+            @pl.when(lon == 2)
+            def _():
+                for t in (0, 1):
+                    hop(c, t, 1, True)
+
+        elif step == 2:
+
+            @pl.when(lon == 2)
+            def _():
+                hop(c, 3, 0, True)
+
+            @pl.when(lon == 1)
+            def _():
+                hop(c, 0, 1, True)
+
+        else:
+            for t in range(4):
+
+                @pl.when(lon == t)
+                def _():
+                    total = acc[c, t]
+                    for side, fits in ((0, t > 0), (1, t < 3)):
+                        if fits:
+                            link(c, t, side).wait_recv()
+                            total = total + lrecv[c, side, t].astype(jnp.float32)
+                    gw_ref[:, c * cols : (c + 1) * cols] = total
+
     refs = (q_s, k_s, v_s, ga, kv_in, dq_ref, att_s, own, dsend, ext)
     for c in range(chunks):
-        for copy in kv_copies[c]:
-            copy.wait_recv()
+        if c + 1 < chunks:
+            pass_on(c + 1)
+        take(c)
 
         @pl.loop(0, CHUNK_HEADS)
         def _(h):
-            attend_head(c * cols + h * HEAD_DIM, h * HEAD_DIM, counts_ref, refs)
+            attend_head(c * cols + h * HEAD_DIM, h * HEAD_DIM, counts, refs)
 
         for copy in d_copies[c]:
             copy.start()
@@ -346,46 +470,63 @@
         stage(0, c)
         if c > 0:
             stage(1, c - 1)
+            if line:
+                chain(0, c - 1)
     stage(1, chunks - 1)
-    for s in range(2, last + 1):
+
+    def join(c):
+        cut = slice(c * cols, (c + 1) * cols)
+        for copy in d_copies[c]:
+            copy.wait_recv()
+        for n, ref in ((0, dk_ref), (1, dv_ref)):
+            ref[:, cut] = (
+                own[n, :, cut]
+                + drecv[0, n, :, cut].astype(jnp.float32)
+                + drecv[1, n, :, cut].astype(jnp.float32)
+            ).astype(jnp.bfloat16)
+
+    if line:
+        chain(0, chunks - 1)
         for c in range(chunks):
-            if s == 2:
-                cut = slice(c * cols, (c + 1) * cols)
-                for copy in d_copies[c]:
-                    copy.wait_recv()
-                for n, ref in ((0, dk_ref), (1, dv_ref)):
-                    ref[:, cut] = (
-                        own[n, :, cut]
-                        + drecv[0, n, :, cut].astype(jnp.float32)
-                        + drecv[1, n, :, cut].astype(jnp.float32)
-                    ).astype(jnp.bfloat16)
-            stage(s, c)
+            chain(1, c)
+        for c in range(chunks):
+            join(c)
+            chain(2, c)
+        for c in range(chunks):
+            chain(3, c)
+    else:
+        for s in range(2, last + 1):
+            for c in range(chunks):
+                stage(s, c)
+        for c in range(chunks):
+            join(c)
     for copy in og_copies:
         copy.wait_send()
     for c in range(chunks):
-        for copy in kv_copies[c] + d_copies[c]:
+        each_kv(c, lambda copy: copy.wait_send())
+        if line:
+            for way in range(2):
+
+                @pl.when(lon == 1 + way)
+                def _():
+                    for n in range(2):
+                        relay(c, n, way).wait_send()
+
+        for copy in d_copies[c]:
             copy.wait_send()
         for s in range(last):
             weight_copy(s, c).wait_send()
+        if line:
+            for t in range(4):
+                pl.when(lon < t)(link(c, t, 0).wait_send)
+                pl.when(lon > t)(link(c, t, 1).wait_send)
 
 
 def local(queries, key_heads, value_heads, out_grad, out_weight, neighbours, slot_valid):
     q, k, v = queries[0], key_heads[0], value_heads[0]
     rows, features = q.shape
-    tiles = rows // TILE
     sizes = tuple(lax.axis_size(axis) for axis in ("lon", "head", "dp"))
     lon_count, head_count, dp_count = sizes
-    tile_total = tiles * lon_count
-    first_tile = lax.axis_index("lon") * tiles
-    own_rows = lax.dynamic_slice_in_dim(neighbours, first_tile, tiles, 0)
-    own_live = lax.dynamic_slice_in_dim(slot_valid, first_tile, tiles, 0)
-    index = first_tile + jnp.arange(tiles, dtype=jnp.int32)
-    offset = (own_rows - index[:, None] + REACH + tile_total) % tile_total
-    span = jnp.arange(WIDE, dtype=jnp.int32)
-    named = (offset[:, :, None] == span) & (own_live > 0)[:, :, None]
-    counts = jnp.sum(named.astype(jnp.float32), axis=1) + (span == REACH).astype(jnp.float32)
-    counts = counts.reshape(-1)
-
     model = out_weight.shape[1]
     cols = CHUNK_HEADS * HEAD_DIM
     chunks = features // cols
@@ -403,7 +544,7 @@
             jax.ShapeDtypeStruct((rows, features), low),
             jax.ShapeDtypeStruct((share, features), wide),
         ],
-        in_specs=[pl.BlockSpec(memory_space=pltpu.SMEM)]
+        in_specs=[pl.BlockSpec(memory_space=pltpu.SMEM)] * 2
         + [pl.BlockSpec(memory_space=pl.ANY)] * 5,
         out_specs=[pl.BlockSpec(memory_space=vmem)] * 4,
         scratch_shapes=[
@@ -433,11 +574,16 @@
             dma((chunks * 4,)),
             dma((chunks * bits,)),
             dma((chunks * bits,)),
+            dma((chunks * 2,)),
+            vmem((chunks, 4, share, cols), low),
+            vmem((chunks, 2, 4, share, cols), low),
+            dma((chunks * 4,)),
+            dma((chunks * 8,)),
         ],
         compiler_params=pltpu.CompilerParams(
             collective_id=0, has_side_effects=True, vmem_limit_bytes=60 * 1024 * 1024
         ),
-    )(counts, q, k, v, out_grad[0], out_weight)
+    )(neighbours, slot_valid, q, k, v, out_grad[0], out_weight)
     return (dq[None], dk[None], dv[None], gw)
 
 

time: 197 us -> 186 us (0.944)
  Pallas kernels: 188 us -> 175 us
    pallas_call x1, Pallas kernels: 188 us -> 175 us  [local(): pl.pallas_call(functools.partial(kernel, sizes), out_shape=[jax.ShapeDtyp...]
    unnamed x10 -> x12, local copies, waits for them, and re-layouts: 6.12 us -> 8.82 us
where the time goes in v3:
time: 186 us; the launch traced here: 184 us
  Pallas kernels  175 us (94%)
  local copies, waits for them, and re-layouts  8.82 us (5%)
    pallas_call x1, Pallas kernels, local(): pl.pallas_call(functools.partial(kernel, sizes), out_shape=[jax.ShapeDtyp...  175 us
    unnamed x12, local copies, waits for them, and re-layouts  8.82 us

profile of v3, /device:TPU:0, one launch (start us, length us, event | category | flops | bytes accessed | tf_op | source)
XLA Modules:
  0.0 184.2 jit_solution(17418664842076398967)
XLA Ops:
  0.6 1.3 copy.11.near_ref
  2.0 1.3 copy.12.valid_ref
  3.3 174.7 %shard_map.102 = (bf16[512,768]{1,0:T(8,128)(2,1)}, bf16[512,768]{1,0:T(8,128)(2,1)}, bf16[512,768]{1,0:T(8,128)(2,1)}, f32[384,768]{1,0:T(8,128)}) custom-call(s32[8,4]{1,0:T(8,128)} %copy.11.near_ref, s32[8,4]{1,0:T(8,128)} %copy.12.valid_ref, bf16[512,768]{1,0:T(8,128)(2,1)} %bitcast.7, bf16[512,768]{1,0:T(8,128)(2,1)} %bitcast.8, ...), custom_call_target="tpu_custom_call" | custom-call | tf_op jit(solution)/shard_map/pallas_call | solution.py:539
  178.0 0.0 copy-start.2
  178.0 2.1 %copy.17 = bf16[1,512,768]{2,1,0:T(8,128)(2,1)} copy(bf16[1,512,768]{2,1,0:T(8,128)(2,1)} %bitcast.13) | data formatting | bytes 1572864
  180.2 0.0 copy-done.2
  180.2 0.0 copy-start.1
  180.2 0.9 copy.18
  181.1 0.5 copy-done.1
  181.6 0.0 copy-start
  181.6 0.9 copy.19
  182.5 0.7 copy-done
  183.2 1.0 copy.20
Async XLA Ops:
  178.0 2.1 %copy-start.2 = (bf16[512,768]{1,0:T(8,128)(2,1)S(1)}, bf16[512,768]{1,0:T(8,128)(2,1)}, u32[]{:S(2)}) copy-start(bf16[512,768]{1,0:T(8,128)(2,1)} %get-tuple-element.9) | copy-start | bytes 2359300
  180.2 1.4 copy-start.1
  181.6 1.6 copy-start

commit v4 on v3

--- a/solution.py
+++ b/solution.py
@@ -106,16 +106,13 @@
 
 def kernel(
     sizes,
-    near_ref,
-    valid_ref,
+    slots_ref,
     q_ref,
     k_ref,
     v_ref,
     og_ref,
     w_ref,
-    dq_ref,
-    dk_ref,
-    dv_ref,
+    grads_ref,
     gw_ref,
     q_s,
     k_s,
@@ -150,6 +147,7 @@
     l_rs,
 ):
     lon_count, head_count, dp_count = sizes
+    dq_ref, dk_ref, dv_ref = (grads_ref.at[n] for n in range(3))
     rows, features = q_s.shape
     model = og_s.shape[1]
     piece = og_ref.shape[0]
@@ -164,9 +162,10 @@
     for i in range(tiles):
         tile = lon * tiles + i
         live = [jnp.float32(1.0 if o == REACH else 0.0) for o in range(WIDE)]
-        for j in range(near_ref.shape[1]):
-            away = lax.rem(near_ref[tile, j] - tile + REACH + tiles * lon_count, tiles * lon_count)
-            used = jnp.where(valid_ref[tile, j] > 0, 1.0, 0.0)
+        for j in range(slots_ref.shape[0]):
+            slot = slots_ref[j, tile]
+            away = lax.rem(slot // 2 - tile + REACH + tiles * lon_count, tiles * lon_count)
+            used = jnp.where(lax.rem(slot, 2) > 0, 1.0, 0.0)
             live = [live[o] + jnp.where(away == o, used, 0.0) for o in range(WIDE)]
         counts.append(live)
     after = {"lon": lax.rem(lon + 1, lon_count)}
@@ -536,17 +535,16 @@
     low, wide = jnp.bfloat16, jnp.float32
     vmem = pltpu.VMEM
     dma = pltpu.SemaphoreType.DMA
-    dq, dk, dv, gw = pl.pallas_call(
+    slots = neighbours.T * 2 + (slot_valid.T > 0).astype(jnp.int32)
+    grads, gw = pl.pallas_call(
         functools.partial(kernel, sizes),
         out_shape=[
-            jax.ShapeDtypeStruct((rows, features), low),
-            jax.ShapeDtypeStruct((rows, features), low),
-            jax.ShapeDtypeStruct((rows, features), low),
+            jax.ShapeDtypeStruct((3, rows, features), low),
             jax.ShapeDtypeStruct((share, features), wide),
         ],
-        in_specs=[pl.BlockSpec(memory_space=pltpu.SMEM)] * 2
+        in_specs=[pl.BlockSpec(memory_space=pltpu.SMEM)]
         + [pl.BlockSpec(memory_space=pl.ANY)] * 5,
-        out_specs=[pl.BlockSpec(memory_space=vmem)] * 4,
+        out_specs=[pl.BlockSpec(memory_space=vmem)] * 2,
         scratch_shapes=[
             vmem((rows, features), low),
             vmem((rows, features), low),
@@ -583,8 +581,8 @@
         compiler_params=pltpu.CompilerParams(
             collective_id=0, has_side_effects=True, vmem_limit_bytes=60 * 1024 * 1024
         ),
-    )(neighbours, slot_valid, q, k, v, out_grad[0], out_weight)
-    return (dq[None], dk[None], dv[None], gw)
+    )(slots, q, k, v, out_grad[0], out_weight)
+    return (grads[0][None], grads[1][None], grads[2][None], gw)
 
 
 def solution(mesh):

time: 186 us -> 182 us (0.978)
  local copies, waits for them, and re-layouts: 8.82 us -> 4.17 us
    unnamed x12 -> x3, local copies, waits for them, and re-layouts: 8.82 us -> 1.02 us
    slice x0 -> x1, local copies, waits for them, and re-layouts: none -> 3.15 us  [local(): return (grads[0][None], grads[1][None], grads[2][None], gw)]
where the time goes in v4:
time: 182 us; the launch traced here: 181 us
  Pallas kernels  175 us (96%)
  local copies, waits for them, and re-layouts  4.17 us (2%)
    pallas_call x1, Pallas kernels, local(): pl.pallas_call(functools.partial(kernel, sizes), out_shape=[jax.ShapeDtyp...  175 us

profile of v4, /device:TPU:0, one launch (start us, length us, event | category | flops | bytes accessed | tf_op | source)
XLA Modules:
  0.0 180.7 jit_solution(17214030034325495857)
XLA Ops:
  0.6 1.3 add_bitcast_fusion.slots_ref
  1.9 174.6 %shard_map.102 = (bf16[3,512,768]{2,1,0:T(8,128)(2,1)}, f32[384,768]{1,0:T(8,128)}) custom-call(s32[4,8]{1,0:T(4,128)} %add_bitcast_fusion.slots_ref, bf16[512,768]{1,0:T(8,128)(2,1)} %bitcast.6, bf16[512,768]{1,0:T(8,128)(2,1)} %bitcast.7, bf16[512,768]{1,0:T(8,128)(2,1)} %bitcast.8, bf16[128,3072]{1,0:T(8,128)(2,1)} %bitcast.9, bf16[768,3072]{1,0:T(8,128)(2,1)} %w_ref.1), custom_call_target="tpu_custom_call" | custom-call | tf_op jit(solution)/shard_map/pallas_call | solution.py:539
  176.5 0.0 copy-start
  176.5 3.2 %fusion = (bf16[1,512,768]{2,1,0:T(8,128)(2,1)}, bf16[1,512,768]{2,1,0:T(8,128)(2,1)}, bf16[1,512,768]{2,1,0:T(8,128)(2,1)}) fusion(bf16[3,512,768]{2,1,0:T(8,128)(2,1)} %get-tuple-element.6), kind=kLoop, calls=%fused_computation.1 | loop fusion | bytes 4718592 | tf_op jit(solution)/shard_map/slice | solution.py:585
  179.7 0.0 copy-done
  179.7 1.0 copy.12
Async XLA Ops:
  176.5 3.2 %copy-start = (f32[384,768]{1,0:T(8,128)S(1)}, f32[384,768]{1,0:T(8,128)}, u32[]{:S(2)}) copy-start(f32[384,768]{1,0:T(8,128)} %get-tuple-element.18) | copy-start | bytes 3538948
